TPU v7x, 32 devices: a whole 2x2x4 slice. The times are simulated.
32 devices in a mesh: expert: 8 (over z, x), tensor: 4 (over y, core).
Axes of the slice: x: 2, y: 2, z: 4, core: 2. Of those that a mesh axis runs over, the one named last changes fastest.
Arguments:
- tokens: bfloat16 [9456, 512], P('expert'), may hold values from -46 to 46
- qkv_weight: bfloat16 [3, 512, 512], P(None, None, 'tensor'), may hold values from -0.25 to 0.25
- out_weight: bfloat16 [512, 512], P('tensor'), may hold values from -2 to 2
- gain_attn: float32 [512], replicated, may hold values from 0.5 to 1.5
- gain_moe: float32 [512], replicated, may hold values from 0.5 to 1.5
- router_weight: bfloat16 [512, 4], replicated, may hold values from -0.1875 to 0.1875
- expert_in: bfloat16 [8, 512, 1024], P('expert', None, 'tensor'), may hold values from -0.25 to 0.25
- expert_out: bfloat16 [8, 1024, 512], P('expert', 'tensor'), may hold values from -0.25 to 0.25
- expert_ids: int32 [9456, 2], P('expert'), may hold values from 0 to 3, all different within a row
- priority: int32 [8, 1182], P('expert'), may hold values from 0 to 1181, each once within a row
- cotangent: bfloat16 [9456, 512], P('expert'), may hold values from -6 to 6
Outputs:
- result: bfloat16 [9456, 512], P('expert')
- grad_tokens: float32 [9456, 512], P('expert')
- grad_qkv: float32 [3, 512, 512], P(None, None, 'tensor')
- grad_out_weight: float32 [512, 512], P('tensor')
- grad_gain_attn: float32 [512], replicated
- grad_gain_moe: float32 [512], replicated
- grad_router: float32 [512, 4], replicated
- grad_expert_in: float32 [8, 512, 1024], P('expert', None, 'tensor')
- grad_expert_out: float32 [8, 1024, 512], P('expert', 'tensor')
- stats: float32 [3], replicated
Inputs may be any that keep to these rules, and one draw needn't show every extreme that they name: `expert_ids`: each token names two different experts; every expert is named by some token. `priority`: each row holds every place 0 to 1181 once; place 0 goes first.
All inputs are finite; a program needn't handle non-finite values.
Results may differ from a plain program's by a relative error of at most 0.013.
The roundings to bfloat16 on the way count: a program that leaves them out, or rounds other values in their place, can miss the bound.
Values may be sent and summed in bfloat16 or wider, within the bound.
No kernel may reach another device: no remote copies, remote signals or barrier semaphores. Data moves between devices by JAX's collectives and lax.ppermute only.
A program may use at most 192 MiB of HBM per device.

v0:
```python
import math

import jax
import jax.numpy as jnp
from jax import lax
from jax.sharding import PartitionSpec as P

HD = 64
LEN = 197


EPSILON = 1e-06
HIGHEST = lax.Precision.HIGHEST


def slot_table(expert_ids, ranking, experts, capacity):
    count = expert_ids.shape[0]
    ordering = jnp.zeros((count,), jnp.int32).at[ranking].set(jnp.arange(count, dtype=jnp.int32))
    expert_iota = jnp.arange(experts, dtype=jnp.int32)
    leading = (expert_ids[:, 0:1] == expert_iota[None, :]).astype(jnp.int32)
    trailing = (expert_ids[:, 1:2] == expert_iota[None, :]).astype(jnp.int32)
    lead_sorted = leading[ordering]
    trail_sorted = trailing[ordering]
    lead_before = (jnp.cumsum(lead_sorted, axis=0) - lead_sorted)[ranking]
    trail_before = (jnp.cumsum(trail_sorted, axis=0) - trail_sorted)[ranking] + jnp.sum(
        leading, axis=0
    )[None, :]
    lead_place = jnp.sum(lead_before * leading, axis=1)
    trail_place = jnp.sum(trail_before * trailing, axis=1)
    placing = jnp.stack([lead_place, trail_place], axis=1)
    return jnp.where(placing < capacity, expert_ids * capacity + placing, experts * capacity)


def norm_parts(values, gain):
    scaling = lax.rsqrt(jnp.mean(values * values, axis=-1, keepdims=True) + EPSILON)
    unit_rows = values * scaling
    return (unit_rows * gain, unit_rows, scaling)


def norm_back(incoming, unit_rows, scaling, gain):
    inner = incoming * gain
    spread_back = scaling * (
        inner - unit_rows * jnp.mean(inner * unit_rows, axis=-1, keepdims=True)
    )
    return (spread_back, jnp.sum(incoming * unit_rows, axis=0))


def pair_tables(slot_block, slot_count):
    slot_iota = jnp.arange(slot_count, dtype=jnp.int32)[None, :]
    return (
        (slot_block[:, 0:1] == slot_iota).astype(jnp.bfloat16),
        (slot_block[:, 1:2] == slot_iota).astype(jnp.bfloat16),
    )


def to_experts(buffer):
    doubled = jnp.repeat(buffer, 2, axis=0)
    moved = lax.all_to_all(doubled, "expert", split_axis=0, concat_axis=0, tiled=True)
    return moved.reshape(moved.shape[0] * moved.shape[1], moved.shape[2])


def tensor_total(summand):
    return lax.psum(summand, "tensor")


def from_experts(rows_back, experts, capacity):
    shaped_back = rows_back.reshape(2 * experts, capacity, rows_back.shape[1])
    moved = lax.all_to_all(shaped_back, "expert", split_axis=0, concat_axis=0, tiled=True)
    width = moved.shape[2]
    halves = jnp.sum(moved.reshape(experts, 2, capacity, width), axis=1)
    return halves.astype(jnp.bfloat16).reshape(experts * capacity, width)


def per_device(
    tokens,
    qkv_weight,
    out_weight,
    gain_attn,
    gain_moe,
    router_weight,
    expert_in,
    expert_out,
    expert_ids,
    priority,
    cotangent,
):
    row_count, features = tokens.shape
    local_width = qkv_weight.shape[2]
    heads_here = local_width // HD
    images = row_count // LEN
    experts = router_weight.shape[1]
    capacity = max(2, 5 * row_count // (2 * experts))
    slot_count = experts * capacity
    block_rows = 2 * LEN
    blocks = row_count // block_rows
    slot_index = slot_table(expert_ids, priority[0], experts, capacity)
    slot_blocks = slot_index.reshape(blocks, block_rows, 2)
    score_root = math.sqrt(HD)
    inputs = tokens.astype(jnp.float32)
    normed_one, unit_one, scale_one = norm_parts(inputs, gain_attn)
    normed_one = normed_one.astype(jnp.bfloat16)
    qkv = jnp.einsum(
        "td,sdf->stf", normed_one, qkv_weight, preferred_element_type=jnp.float32
    ).astype(jnp.bfloat16)
    shaped = qkv.reshape(3, images, LEN, heads_here, HD)
    scores = (
        jnp.einsum("gqhe,gkhe->ghqk", shaped[0], shaped[1], preferred_element_type=jnp.float32)
        / score_root
    )
    row_peak = jnp.max(scores, axis=-1, keepdims=True)
    weights = jnp.exp(scores - row_peak)
    weight_total = jnp.sum(weights, axis=-1, keepdims=True)
    probs = weights / weight_total
    log_total = row_peak + jnp.log(weight_total)
    head_rows = (
        jnp.einsum(
            "ghqk,gkhe->gqhe",
            probs.astype(jnp.bfloat16),
            shaped[2],
            preferred_element_type=jnp.float32,
        )
        .reshape(row_count, local_width)
        .astype(jnp.bfloat16)
    )
    attn = lax.psum(jnp.dot(head_rows, out_weight, preferred_element_type=jnp.float32), "tensor")
    residual = inputs + attn
    normed_two, unit_two, scale_two = norm_parts(residual, gain_moe)
    normed_two = normed_two.astype(jnp.bfloat16)
    logits = jnp.dot(normed_two, router_weight, preferred_element_type=jnp.float32)
    expert_iota = jnp.arange(experts, dtype=jnp.int32)
    choosing = (expert_ids[:, :, None] == expert_iota[None, None, :]).astype(jnp.float32)
    chosen = jnp.sum(choosing * logits[:, None, :], axis=2)
    gates = jax.nn.softmax(chosen, axis=1)

    def collect(carry, element):
        leading, trailing = pair_tables(element[0], slot_count)
        return (
            carry
            + jnp.einsum(
                "tc,td->cd", leading + trailing, element[1], preferred_element_type=jnp.float32
            ),
            None,
        )

    dispatched, ignored = lax.scan(
        collect,
        jnp.zeros((slot_count, features), jnp.float32),
        (slot_blocks, normed_two.reshape(blocks, block_rows, features)),
    )
    dispatched = dispatched.astype(jnp.bfloat16).reshape(experts, capacity, features)
    received = to_experts(dispatched)
    pre_act = jnp.dot(received, expert_in[0], preferred_element_type=jnp.float32)
    activated = jax.nn.gelu(pre_act, approximate=False).astype(jnp.bfloat16)
    returned = from_experts(
        tensor_total(jnp.dot(activated, expert_out[0], preferred_element_type=jnp.float32)),
        experts,
        capacity,
    )
    grad_y = cotangent.astype(jnp.float32)

    def combine(carry, element):
        slot_block, gate_block, grad_block = element
        leading, trailing = pair_tables(slot_block, slot_count)
        got_lead = jnp.dot(leading, returned, preferred_element_type=jnp.float32)
        got_trail = jnp.dot(trailing, returned, preferred_element_type=jnp.float32)
        mixed = gate_block[:, 0:1] * got_lead + gate_block[:, 1:2] * got_trail
        gate_grad = jnp.stack(
            [jnp.sum(grad_block * got_lead, axis=1), jnp.sum(grad_block * got_trail, axis=1)],
            axis=1,
        )
        carry = carry + jnp.einsum(
            "tc,td->cd",
            leading,
            (gate_block[:, 0:1] * grad_block).astype(jnp.bfloat16),
            preferred_element_type=jnp.float32,
        )
        carry = carry + jnp.einsum(
            "tc,td->cd",
            trailing,
            (gate_block[:, 1:2] * grad_block).astype(jnp.bfloat16),
            preferred_element_type=jnp.float32,
        )
        return (carry, (mixed, gate_grad))

    grad_slots, (moe, gate_grad) = lax.scan(
        combine,
        jnp.zeros((slot_count, features), jnp.float32),
        (
            slot_blocks,
            gates.reshape(blocks, block_rows, 2),
            grad_y.reshape(blocks, block_rows, features),
        ),
    )
    moe = moe.reshape(row_count, features)
    gate_grad = gate_grad.reshape(row_count, 2)
    result = (residual + moe).astype(jnp.bfloat16)
    grad_rows = to_experts(grad_slots.astype(jnp.bfloat16).reshape(experts, capacity, features))
    grad_act = jnp.einsum("rd,fd->rf", grad_rows, expert_out[0], preferred_element_type=jnp.float32)
    ignored, gelu_back = jax.vjp(lambda values: jax.nn.gelu(values, approximate=False), pre_act)
    grad_pre = gelu_back(grad_act)[0].astype(jnp.bfloat16)
    grad_expert_out = jnp.einsum(
        "rf,rd->fd", activated, grad_rows, preferred_element_type=jnp.float32
    )
    grad_expert_in = jnp.einsum("rd,rf->df", received, grad_pre, preferred_element_type=jnp.float32)
    grad_sent = from_experts(
        tensor_total(
            jnp.einsum("rf,df->rd", grad_pre, expert_in[0], preferred_element_type=jnp.float32)
        ),
        experts,
        capacity,
    )
    grad_choice = gates * (gate_grad - jnp.sum(gates * gate_grad, axis=1, keepdims=True))
    grad_logits = jnp.sum(choosing * grad_choice[:, :, None], axis=1)
    grad_router = jnp.einsum(
        "td,te->de", normed_two.astype(jnp.float32), grad_logits, precision=HIGHEST
    )
    router_back = jnp.einsum(
        "te,de->td", grad_logits, router_weight.astype(jnp.float32), precision=HIGHEST
    )

    def spread_rows(slot_block):
        leading, trailing = pair_tables(slot_block, slot_count)
        return jnp.dot(leading + trailing, grad_sent, preferred_element_type=jnp.float32)

    grad_normed_two = lax.map(spread_rows, slot_blocks).reshape(row_count, features) + router_back
    residual_back, grad_gain_moe = norm_back(grad_normed_two, unit_two, scale_two, gain_moe)
    grad_residual = grad_y + residual_back
    grad_attn = grad_residual.astype(jnp.bfloat16)
    grad_out_weight = jnp.einsum(
        "tf,td->fd", head_rows, grad_attn, preferred_element_type=jnp.float32
    )
    grad_heads = jnp.einsum("td,fd->tf", grad_attn, out_weight, preferred_element_type=jnp.float32)
    grad_heads = grad_heads.astype(jnp.bfloat16).reshape(images, LEN, heads_here, HD)
    scores_again = (
        jnp.einsum("gqhe,gkhe->ghqk", shaped[0], shaped[1], preferred_element_type=jnp.float32)
        / score_root
    )
    probs_again = jnp.exp(scores_again - log_total)
    grad_probs = jnp.einsum(
        "gqhe,gkhe->ghqk", grad_heads, shaped[2], preferred_element_type=jnp.float32
    )
    grad_scores = (
        probs_again * (grad_probs - jnp.sum(probs_again * grad_probs, axis=-1, keepdims=True))
    ).astype(jnp.bfloat16)
    grad_values = jnp.einsum(
        "ghqk,gqhe->gkhe",
        probs_again.astype(jnp.bfloat16),
        grad_heads,
        preferred_element_type=jnp.float32,
    )
    grad_queries = (
        jnp.einsum("ghqk,gkhe->gqhe", grad_scores, shaped[1], preferred_element_type=jnp.float32)
        / score_root
    )
    grad_keys = (
        jnp.einsum("ghqk,gqhe->gkhe", grad_scores, shaped[0], preferred_element_type=jnp.float32)
        / score_root
    )
    grad_qkv_rows = (
        jnp.stack([grad_queries, grad_keys, grad_values])
        .reshape(3, row_count, local_width)
        .astype(jnp.bfloat16)
    )
    grad_qkv = jnp.einsum(
        "td,stf->sdf", normed_one, grad_qkv_rows, preferred_element_type=jnp.float32
    )
    grad_normed_one = lax.psum(
        jnp.einsum("stf,sdf->td", grad_qkv_rows, qkv_weight, preferred_element_type=jnp.float32),
        "tensor",
    )
    input_back, grad_gain_attn = norm_back(grad_normed_one, unit_one, scale_one, gain_attn)
    grad_tokens = grad_residual + input_back
    squares = jnp.stack([jnp.sum(inputs * inputs), jnp.sum(attn * attn), jnp.sum(moe * moe)])
    summed = lax.psum(
        (grad_qkv, grad_out_weight, grad_gain_attn, grad_gain_moe, grad_router, squares), "expert"
    )
    entry_count = float(row_count * features * lax.axis_size("expert"))
    stats = jnp.sqrt(summed[5] / entry_count)
    return (
        result,
        grad_tokens,
        summed[0],
        summed[1],
        summed[2],
        summed[3],
        summed[4],
        grad_expert_in[None],
        grad_expert_out[None],
        stats,
    )


def solution(mesh):
    in_specs = (
        P("expert", None),
        P(None, None, "tensor"),
        P("tensor", None),
        P(),
        P(),
        P(),
        P("expert", None, "tensor"),
        P("expert", "tensor", None),
        P("expert", None),
        P("expert", None),
        P("expert", None),
    )
    out_specs = (
        P("expert", None),
        P("expert", None),
        P(None, None, "tensor"),
        P("tensor", None),
        P(),
        P(),
        P(),
        P("expert", None, "tensor"),
        P("expert", "tensor", None),
        P(),
    )
    return jax.shard_map(
        per_device, mesh=mesh, in_specs=in_specs, out_specs=out_specs, check_vma=False
    )
```

profile of v0, /device:TPU:0, one launch (start us, length us, event | category | flops | bytes accessed | tf_op | source)
XLA Modules:
  0.0 1753.5 jit_solution(8087961302006802896)
XLA Ops:
  20.1 6.7 scatter_custom_fusion
  42.9 36.6 %all-reduce.10.cloned.1.call-done = f32[1182,512]{1,0:T(8,128)} async-done(((f32[1182,512]{1,0:T(8,128)}), f32[1182,512]{1,0:T(8,128)}) %all-reduce.10.cloned.1.call-update) | async-done | bytes 2420752 | tf_op jit(solution)/shard_map/psum | solution.py:125
  79.5 3.1 multiply_reduce_fusion.5
  85.4 19.7 %while.37 = (s32[]{:T(128)}, f32[2952,512]{1,0:T(8,128)}, s32[3,394,2]{1,2,0:T(2,128)S(1)}, bf16[3,394,512]{2,1,0:T(8,128)(2,1)S(1)}, s32[]{:T(128)}, /*index=5*/s32[]{:T(128)}) while((s32[]{:T(128)}, f32[2952,512]{1,0:T(8,128)}, s32[3,394,2]{1,2,0:T(2,128)S(1)}, bf16[3,394,512]{2,1,0:T(8,128)(2,1)S(1)}, s32[]{:T(128)}, ...), condition=%wide.region_17.18_spmd.clone, body=%wide.region_16.17_spmd.clone.sunk | while | flops 1203329664 | bytes 12517783 | solution.py:145
  85.4 4.8 select_add_fusion.3
  90.2 7.5 select_add_fusion.3
  97.7 7.5 select_add_fusion.3
  105.2 4.8 convert_element_type.113
  113.1 140.2 %all_to_all.20 = bf16[8,738,512]{2,1,0:T(8,128)(2,1)} all-to-all(bf16[8,738,512]{2,1,0:T(8,128)(2,1)S(1)} %bitcast.197), channel_id=1, replica_groups=mesh['expert'=8,'tensor'=4] {'expert'}, dimensions={0} | all-to-all | bytes 12091392 | tf_op jit(solution)/shard_map/all_to_all | solution.py:58
  253.3 5.3 reshape.273
  258.7 16.8 multiply_convert_fusion
  277.1 6.1 fusion.85
  283.1 12.0 reshape.274
  295.2 212.1 %all-reduce.12.cloned.1.call-done = f32[8,738,512]{2,1,0:T(8,128)} async-done(((f32[8,738,512]{2,1,0:T(8,128)}), f32[8,738,512]{2,1,0:T(8,128)}) %all-reduce.12.cloned.1.call-update) | async-done | bytes 12091408 | tf_op jit(solution)/shard_map/psum | solution.py:63
  507.3 5.5 all-to-all-start.1
  516.5 260.5 %all-to-all-done.1 = f32[8,738,512]{2,1,0:T(8,128)} async-done(((f32[8,738,512]{2,1,0:T(8,128)}), f32[8,738,512]{2,1,0:T(8,128)}, u32[]{:S(2)}, u32[]{:S(2)}) %all-to-all-start.1) | async-done | bytes 12091424 | tf_op jit(solution)/shard_map/all_to_all | solution.py:68
  777.1 8.6 bitcast_reduce_fusion.1
  785.6 4.3 convert_element_type.116
  791.7 58.5 %while.38 = (s32[]{:T(128)}, f32[2952,512]{1,0:T(8,128)}, f32[3,394,512]{2,1,0:T(8,128)}, f32[3,394,2]{1,0,2:T(4,128)}, s32[3,394,2]{1,2,0:T(2,128)S(1)}, /*inde...) while((s32[]{:T(128)}, f32[2952,512]{1,0:T(8,128)}, ...), condition=%wide.region_23.24_spmd.clone, body=%wide.region_20.23_spmd.clone.sunk | while | flops 4775414272 | bytes 49687696 | solution.py:185
  791.9 4.7 fusion.174
  796.6 7.9 fusion.175
  810.2 4.7 fusion.174
  814.9 9.7 fusion.175
  830.2 4.7 fusion.174
  834.9 9.7 fusion.175
  850.2 4.7 convert_element_type.118
  858.1 138.4 %all_to_all.21 = bf16[8,738,512]{2,1,0:T(8,128)(2,1)} all-to-all(bf16[8,738,512]{2,1,0:T(8,128)(2,1)S(1)} %bitcast.198), channel_id=1, replica_groups=mesh['expert'=8,'tensor'=4] {'expert'}, dimensions={0} | all-to-all | bytes 12091392 | tf_op jit(solution)/shard_map/all_to_all | solution.py:58
  996.5 5.3 reshape.279
  1001.9 8.1 add_convert_fusion
  1011.6 6.2 fusion.89
  1017.8 11.9 reshape.280
  1029.8 212.5 %all-reduce.14.cloned.1.call-done = f32[8,738,512]{2,1,0:T(8,128)} async-done(((f32[8,738,512]{2,1,0:T(8,128)}), f32[8,738,512]{2,1,0:T(8,128)}) %all-reduce.14.cloned.1.call-update) | async-done | bytes 12091408 | tf_op jit(solution)/shard_map/psum | solution.py:63
  1242.3 5.5 all-to-all-start.3
  1248.1 3.3 reshape.276
  1251.5 260.6 %all-to-all-done.3 = f32[8,738,512]{2,1,0:T(8,128)} async-done(((f32[8,738,512]{2,1,0:T(8,128)}), f32[8,738,512]{2,1,0:T(8,128)}, u32[]{:S(2)}, u32[]{:S(2)}) %all-to-all-start.3) | async-done | bytes 12091424 | tf_op jit(solution)/shard_map/all_to_all | solution.py:68
  1512.1 6.4 bitcast_reduce_fusion
  1522.6 13.2 while.36
  1523.0 4.2 fusion.164
  1527.3 4.3 fusion.164
  1531.6 4.2 fusion.164
  1535.8 3.5 reshape.282
  1539.4 3.9 multiply_reduce_fusion.3
  1568.8 6.4 convolution_bitcast_fusion.2
  1577.9 62.0 %all-reduce.18.cloned.1.call-done = (f32[3,512,128]{1,2,0:T(8,128)}, f32[128,512]{1,0:T(8,128)}) async-done(((f32[3,512,128]{1,2,0:T(8,128)}, f32[128,512]{1,0:T(8,128)}), (f32[3,512,128]{1,2,0:T(8,128)}, f32[128,512]{1,0:T(8,128)})) %all-reduce.18.cloned.1.call-update) | async-done | bytes 1048592 | tf_op jit(solution)/shard_map/psum | solution.py:274
  1642.2 56.4 %all-reduce.16.cloned.1.call-done = f32[1182,512]{1,0:T(8,128)} async-done(((f32[1182,512]{1,0:T(8,128)}), f32[1182,512]{1,0:T(8,128)}) %all-reduce.16.cloned.1.call-update) | async-done | bytes 2420752 | tf_op jit(solution)/shard_map/psum | solution.py:267
  1698.6 3.8 fusion.61
  1704.4 37.1 %all-reduce.2 = (f32[512]{0:T(512)}, f32[512]{0:T(512)}, f32[512,4]{0,1:T(4,128)}, f32[3]{0:T(128)S(1)}) all-reduce(f32[512]{0:T(512)S(1)} %get-tuple-element.211, f32[512]{0:T(512)S(1)} %get-tuple-element.209, f32[512,4]{0,1:T(4,128)S(1)} %fusion.108, f32[3]{0:T(128)S(1)} %pad_maximum_fusion), channel_id=1, replica_groups=mesh['expert'=8,'tensor'=4] {'expert'}, use_global_device_ids=true, to_apply=%region_37.38 | all-reduce | flops 3075 | bytes 24600 | tf_op jit(solution)/shard_map/psum | solution.py:274
  1742.0 4.1 fusion.60
  (275 shorter events, 101.1 us)
Async XLA Ops:
  7.2 72.4 %all-reduce.10.cloned.1.call-start = ((), (), s32[]{:S(2)}) async-start(), calls=%async_computation.4 | async-start | bytes 4849664 | tf_op jit(solution)/shard_map/psum | solution.py:125
  8.9 2.2 copy-start.41
  12.3 2.9 copy-start.17
  13.4 2.3 copy-start.19
  14.6 2.7 copy-start.26
  15.2 2.1 copy-start.1
  15.2 2.1 copy-start.39
  17.6 2.5 copy-start.51
  17.6 9.3 copy-start.36
  18.0 8.9 copy-start.22
  19.9 487.4 %all-reduce.12.cloned.1.call-start = ((), (), s32[]{:S(2)}) async-start(), calls=%async_computation.5 | async-start | bytes 24379392 | tf_op jit(solution)/shard_map/psum | solution.py:63
  39.4 40.1 %copy-start.11 = (bf16[1182,512]{1,0:T(8,128)(2,1)S(1)}, bf16[1182,512]{1,0:T(8,128)(2,1)}, u32[]{:S(2)}) copy-start(bf16[1182,512]{1,0:T(8,128)(2,1)} %param.17) | copy-start | bytes 3631108
  42.9 41.2 %copy-start.46 = (f32[512]{0:T(512)S(1)}, f32[512]{0:T(512)}, u32[]{:S(2)}) copy-start(f32[512]{0:T(512)} %param.21) | copy-start | bytes 6148
  82.6 2.0 copy-start.37
  253.3 5.3 copy-start.33
  258.7 18.4 %copy-start.31 = (bf16[1,256,512]{2,1,0:T(8,128)(2,1)S(1)}, bf16[1,256,512]{2,1,0:T(8,128)(2,1)}, u32[]{:S(2)}) copy-start(bf16[1,256,512]{2,1,0:T(8,128)(2,1)} %param.24) | copy-start | bytes 786436
  507.3 269.8 %all-to-all-start.1 = ((f32[8,738,512]{2,1,0:T(8,128)}), f32[8,738,512]{2,1,0:T(8,128)}, u32[]{:S(2)}, u32[]{:S(2)}) async-start(f32[8,738,512]{2,1,0:T(8,128)} %all-reduce.12.cloned.1.call-done), calls=%async_computation.1 | async-start | bytes 24379392 | tf_op jit(solution)/shard_map/all_to_all | solution.py:68
  512.8 729.5 %all-reduce.14.cloned.1.call-start = ((), (), s32[]{:S(2)}) async-start(), calls=%async_computation.6 | async-start | bytes 24379392 | tf_op jit(solution)/shard_map/psum | solution.py:63
  796.6 7.9 copy-start.21
  814.9 9.7 copy-start.21
  834.9 9.7 copy-start.21
  996.5 5.4 copy-start.32
  1001.9 9.7 copy-start.34
  1029.8 218.1 %copy-start.40 = (f32[6,2,197]{2,1,0:T(2,128)S(1)}, f32[6,2,197]{2,1,0:T(2,128)}, u32[]{:S(2)}) copy-start(f32[6,2,197]{2,1,0:T(2,128)} %copy-done.39) | copy-start | bytes 28372
  1029.8 218.1 %copy-start.45 = (f32[6,2,197]{2,1,0:T(2,128)S(1)}, f32[6,2,197]{2,1,0:T(2,128)}, u32[]{:S(2)}) copy-start(f32[6,2,197]{2,1,0:T(2,128)} %copy-done.44) | copy-start | bytes 28372
  1029.8 218.1 %copy-start.43 = (f32[3,394,2]{1,0,2:T(4,128)S(1)}, f32[3,394,2]{1,0,2:T(4,128)}, u32[]{:S(2)}) copy-start(f32[3,394,2]{1,0,2:T(4,128)} %get-tuple-element.102) | copy-start | bytes 28372
  1242.3 269.8 %all-to-all-start.3 = ((f32[8,738,512]{2,1,0:T(8,128)}), f32[8,738,512]{2,1,0:T(8,128)}, u32[]{:S(2)}, u32[]{:S(2)}) async-start(f32[8,738,512]{2,1,0:T(8,128)} %all-reduce.14.cloned.1.call-done), calls=%async_computation.3 | async-start | bytes 24379392 | tf_op jit(solution)/shard_map/all_to_all | solution.py:68
  1247.8 392.1 %all-reduce.18.cloned.1.call-start = ((), (), s32[]{:S(2)}) async-start(), calls=%async_computation.8 | async-start | bytes 2097152 | tf_op jit(solution)/shard_map/psum | solution.py:274
  1535.8 3.5 copy-start.4
  1535.8 3.5 copy-start.38
  1535.8 3.5 copy-start.47
  1535.8 3.5 copy-start.49
  1539.4 4.0 copy-start.15
  1539.4 4.0 copy-start.16
  1543.4 3.3 copy-start.30
  1545.2 4.8 copy-start.2
  1553.2 2.8 copy-start.28
  1557.2 3.7 copy-start.12
  1557.2 3.6 copy-start.42
  1557.2 3.6 copy-start.50
  1560.9 5.0 copy-start.14
  1562.7 135.9 %all-reduce.16.cloned.1.call-start = ((), (), s32[]{:S(2)}) async-start(), calls=%async_computation.7 | async-start | bytes 4849664 | tf_op jit(solution)/shard_map/psum | solution.py:267
  1562.9 3.6 copy-start.25
  1566.5 8.8 slice-start
  1568.8 6.4 slice-start.1
  1568.8 6.4 copy-start.10
  1577.9 164.1 %copy-start.7 = (f32[1182,512]{1,0:T(8,128)S(1)}, f32[1182,512]{1,0:T(8,128)}, u32[]{:S(2)}) copy-start(f32[1182,512]{1,0:T(8,128)} %copy-done.5) | copy-start | bytes 7262212
  1742.0 4.1 copy-start.35
  (15 other events, 20.9 us)
Sparse Core Ops, SparseCore 0:
  20.1 59.4 all-reduce.9
  295.3 211.9 all-reduce.11
  1029.9 212.4 all-reduce.13
  1562.8 77.0 all-reduce.17
  1642.1 56.4 all-reduce.15
where the time goes:
time: 1760 us; the launch traced here: 1750 us
  waiting for transfers between devices  1100 us (62%)
  blocking collectives  316 us (18%)
  matrix products  152 us (9%)
  local copies, waits for them, and re-layouts  107 us (6%)
  other arithmetic  51.3 us (3%)
    all_to_all x2, waiting for transfers between devices, from_experts(): lax.all_to_all(shaped_back, 'expert', split_axis=0, concat_axis=0, tiled=...  521 us
    psum x2, waiting for transfers between devices, tensor_total(): return lax.psum(summand, 'tensor')  425 us
    all_to_all x2, blocking collectives, to_experts(): lax.all_to_all(doubled, 'expert', split_axis=0, concat_axis=0, tiled=True)  279 us
    psum x1, waiting for transfers between devices, per_device(): lax.psum((grad_qkv, grad_out_weight, grad_gain_attn, grad_gain_moe, grad_...  62 us
    psum x1, waiting for transfers between devices, per_device(): lax.psum(jnp.einsum('stf,sdf->td', grad_qkv_rows, qkv_weight, preferred_e...  56.4 us
    psum x1, blocking collectives, per_device(): lax.psum((grad_qkv, grad_out_weight, grad_gain_attn, grad_gain_moe, grad_...  37.1 us
    psum x1, waiting for transfers between devices, per_device(): lax.psum(jnp.dot(head_rows, out_weight, preferred_element_type=jnp.float3...  36.6 us
  transfers between devices with their start and end apart: 7, of which 7 were waited for; matrix products, arithmetic and copies ran while one was open for 3% of the time, Pallas kernels for 0%

commit v1 on v0

--- a/solution.py
+++ b/solution.py
@@ -3,6 +3,8 @@
 import jax
 import jax.numpy as jnp
 from jax import lax
+from jax.experimental import pallas as pl
+from jax.experimental.pallas import tpu as pltpu
 from jax.sharding import PartitionSpec as P
 
 HD = 64
@@ -71,7 +73,7 @@
     return halves.astype(jnp.bfloat16).reshape(experts * capacity, width)
 
 
-def per_device(
+def per_device_slots(
     tokens,
     qkv_weight,
     out_weight,
@@ -290,6 +292,274 @@
     )
 
 
+MOST_DENSE = 8
+
+
+def dense_experts_kernel(
+    x_ref, dy_ref, gate_ref, win_ref, wout_ref,
+    moe_ref, dx_ref, gg_ref, gwin_ref, gwout_ref,
+    moe_acc, dx_acc, gact_ref, gpre_ref,
+):
+    step = pl.program_id(0)
+    chosen = step // 2
+
+    @pl.when(step == 0)
+    def _():
+        moe_acc[...] = jnp.zeros_like(moe_acc)
+        dx_acc[...] = jnp.zeros_like(dx_acc)
+        gg_ref[...] = jnp.zeros_like(gg_ref)
+
+    rows = x_ref.shape[0]
+    chunk = rows // 4
+    win = win_ref[0]
+    wout = wout_ref[0]
+    for c in range(4):
+        part = pl.ds(c * chunk, chunk)
+        pre = jnp.dot(x_ref[part, :], win, preferred_element_type=jnp.float32)
+        back = lax.dot_general(
+            dy_ref[part, :], wout, (((1,), (1,)), ((), ())), preferred_element_type=jnp.float32
+        )
+        half = 0.5 + 0.5 * lax.erf(pre * math.sqrt(0.5))
+        act = pre * half
+        slope = half + pre * (jnp.exp(pre * pre * -0.5) * (1.0 / math.sqrt(2.0 * math.pi)))
+        lane = lax.broadcasted_iota(jnp.int32, (chunk, gate_ref.shape[1]), 1)
+        mine = lane == chosen
+        gate = jnp.sum(jnp.where(mine, gate_ref[part, :], 0.0), axis=1, keepdims=True)
+        act = act.astype(jnp.bfloat16).astype(jnp.float32)
+        seen = jnp.sum(act * back, axis=1, keepdims=True)
+        gg_ref[part, :] = gg_ref[part, :] + jnp.where(mine, seen, 0.0)
+        gact_ref[part, :] = (gate * act).astype(jnp.bfloat16)
+        gpre_ref[part, :] = (gate * back * slope).astype(jnp.bfloat16)
+    gact = gact_ref[...]
+    gpre = gpre_ref[...]
+    moe_acc[...] += jnp.dot(gact, wout, preferred_element_type=jnp.float32)
+    dx_acc[...] += lax.dot_general(
+        gpre, win, (((1,), (1,)), ((), ())), preferred_element_type=jnp.float32
+    )
+    gwin_ref[0] = lax.dot_general(
+        x_ref[...], gpre, (((0,), (0,)), ((), ())), preferred_element_type=jnp.float32
+    ).astype(gwin_ref.dtype)
+    gwout_ref[0] = lax.dot_general(
+        gact, dy_ref[...], (((0,), (0,)), ((), ())), preferred_element_type=jnp.float32
+    ).astype(gwout_ref.dtype)
+
+    @pl.when(step == pl.num_programs(0) - 1)
+    def _():
+        moe_ref[...] = moe_acc[...].astype(moe_ref.dtype)
+        dx_ref[...] = dx_acc[...].astype(dx_ref.dtype)
+
+
+def dense_experts(x, dy, gate, win, wout):
+    rows, features = x.shape
+    halves, _, hidden = win.shape
+    experts = gate.shape[1]
+    whole = lambda shape: pl.BlockSpec(shape, lambda j: (0,) * len(shape))
+    return pl.pallas_call(
+        dense_experts_kernel,
+        grid=(halves,),
+        in_specs=[
+            whole((rows, features)),
+            whole((rows, features)),
+            whole((rows, experts)),
+            pl.BlockSpec((1, features, hidden), lambda j: (j, 0, 0)),
+            pl.BlockSpec((1, hidden, features), lambda j: (j, 0, 0)),
+        ],
+        out_specs=[
+            whole((rows, features)),
+            whole((rows, features)),
+            whole((rows, experts)),
+            pl.BlockSpec((1, features, hidden), lambda j: (j, 0, 0)),
+            pl.BlockSpec((1, hidden, features), lambda j: (j, 0, 0)),
+        ],
+        out_shape=[
+            jax.ShapeDtypeStruct((rows, features), jnp.bfloat16),
+            jax.ShapeDtypeStruct((rows, features), jnp.bfloat16),
+            jax.ShapeDtypeStruct((rows, experts), jnp.float32),
+            jax.ShapeDtypeStruct((halves, features, hidden), jnp.bfloat16),
+            jax.ShapeDtypeStruct((halves, hidden, features), jnp.bfloat16),
+        ],
+        scratch_shapes=[
+            pltpu.VMEM((rows, features), jnp.float32),
+            pltpu.VMEM((rows, features), jnp.float32),
+            pltpu.VMEM((rows, hidden), jnp.bfloat16),
+            pltpu.VMEM((rows, hidden), jnp.bfloat16),
+        ],
+        name="dense_experts",
+    )(x, dy, gate, win, wout)
+
+
+def kept_pairs(expert_ids, ranking, experts, capacity):
+    iota = jnp.arange(experts, dtype=jnp.int32)[None, :]
+    leading = (expert_ids[:, 0:1] == iota).astype(jnp.bfloat16)
+    trailing = (expert_ids[:, 1:2] == iota).astype(jnp.bfloat16)
+    earlier = (ranking[None, :] < ranking[:, None]).astype(jnp.bfloat16)
+    before = jnp.dot(
+        earlier, jnp.concatenate([leading, trailing], axis=1), preferred_element_type=jnp.float32
+    )
+    lead_f = leading.astype(jnp.float32)
+    trail_f = trailing.astype(jnp.float32)
+    lead_place = jnp.sum(before[:, :experts] * lead_f, axis=1)
+    trail_place = jnp.sum((before[:, experts:] + jnp.sum(lead_f, axis=0)) * trail_f, axis=1)
+    kept = jnp.stack([lead_place, trail_place], axis=1) < capacity
+    return kept.astype(jnp.float32), lead_f, trail_f
+
+
+def per_device_dense(
+    tokens,
+    qkv_weight,
+    out_weight,
+    gain_attn,
+    gain_moe,
+    router_weight,
+    expert_in,
+    expert_out,
+    expert_ids,
+    priority,
+    cotangent,
+):
+    row_count, features = tokens.shape
+    local_width = qkv_weight.shape[2]
+    heads_here = local_width // HD
+    images = row_count // LEN
+    experts = router_weight.shape[1]
+    capacity = max(2, 5 * row_count // (2 * experts))
+    padded = -(-row_count // 32) * 32
+    win_all = lax.all_gather(expert_in[0], "expert")
+    wout_all = lax.all_gather(expert_out[0], "expert")
+    kept, leading, trailing = kept_pairs(expert_ids, priority[0], experts, capacity)
+    score_root = math.sqrt(HD)
+    inputs = tokens.astype(jnp.float32)
+    normed_one, unit_one, scale_one = norm_parts(inputs, gain_attn)
+    normed_one = normed_one.astype(jnp.bfloat16)
+    qkv = jnp.einsum(
+        "td,sdf->stf", normed_one, qkv_weight, preferred_element_type=jnp.float32
+    ).astype(jnp.bfloat16)
+    shaped = qkv.reshape(3, images, LEN, heads_here, HD)
+    scores = (
+        jnp.einsum("gqhe,gkhe->ghqk", shaped[0], shaped[1], preferred_element_type=jnp.float32)
+        / score_root
+    )
+    row_peak = jnp.max(scores, axis=-1, keepdims=True)
+    weights = jnp.exp(scores - row_peak)
+    weight_total = jnp.sum(weights, axis=-1, keepdims=True)
+    probs = weights / weight_total
+    log_total = row_peak + jnp.log(weight_total)
+    head_rows = (
+        jnp.einsum(
+            "ghqk,gkhe->gqhe",
+            probs.astype(jnp.bfloat16),
+            shaped[2],
+            preferred_element_type=jnp.float32,
+        )
+        .reshape(row_count, local_width)
+        .astype(jnp.bfloat16)
+    )
+    attn = lax.psum(
+        jnp.dot(head_rows, out_weight, preferred_element_type=jnp.float32).astype(jnp.bfloat16),
+        "tensor",
+    ).astype(jnp.float32)
+    residual = inputs + attn
+    normed_two, unit_two, scale_two = norm_parts(residual, gain_moe)
+    normed_two = normed_two.astype(jnp.bfloat16)
+    logits = jnp.dot(normed_two, router_weight, preferred_element_type=jnp.float32)
+    chosen = jnp.stack(
+        [jnp.sum(leading * logits, axis=1), jnp.sum(trailing * logits, axis=1)], axis=1
+    )
+    gates = jax.nn.softmax(chosen, axis=1)
+    kept_gates = gates * kept
+    spread_gates = leading * kept_gates[:, 0:1] + trailing * kept_gates[:, 1:2]
+    pad = lambda v: jnp.pad(v, ((0, padded - row_count), (0, 0)))
+    moe_part, back_part, gate_part, grad_in, grad_out = dense_experts(
+        pad(normed_two), pad(cotangent), pad(spread_gates), win_all, wout_all
+    )
+    back_sum, gate_sum = lax.psum((back_part, gate_part), "tensor")
+    moe = lax.psum(moe_part, "tensor")[:row_count].astype(jnp.float32)
+    grad_expert_in = lax.psum_scatter(grad_in, "expert", scatter_dimension=0, tiled=True)
+    grad_expert_out = lax.psum_scatter(grad_out, "expert", scatter_dimension=0, tiled=True)
+    grad_y = cotangent.astype(jnp.float32)
+    gate_sum = gate_sum[:row_count]
+    gate_grad = kept * jnp.stack(
+        [jnp.sum(leading * gate_sum, axis=1), jnp.sum(trailing * gate_sum, axis=1)], axis=1
+    )
+    result = (residual + moe).astype(jnp.bfloat16)
+    grad_choice = gates * (gate_grad - jnp.sum(gates * gate_grad, axis=1, keepdims=True))
+    grad_logits = leading * grad_choice[:, 0:1] + trailing * grad_choice[:, 1:2]
+    grad_router = jnp.einsum(
+        "td,te->de", normed_two.astype(jnp.float32), grad_logits, precision=HIGHEST
+    )
+    router_back = jnp.einsum(
+        "te,de->td", grad_logits, router_weight.astype(jnp.float32), precision=HIGHEST
+    )
+    grad_normed_two = back_sum[:row_count].astype(jnp.float32) + router_back
+    residual_back, grad_gain_moe = norm_back(grad_normed_two, unit_two, scale_two, gain_moe)
+    grad_residual = grad_y + residual_back
+    grad_attn = grad_residual.astype(jnp.bfloat16)
+    grad_out_weight = jnp.einsum(
+        "tf,td->fd", head_rows, grad_attn, preferred_element_type=jnp.float32
+    )
+    grad_heads = jnp.einsum("td,fd->tf", grad_attn, out_weight, preferred_element_type=jnp.float32)
+    grad_heads = grad_heads.astype(jnp.bfloat16).reshape(images, LEN, heads_here, HD)
+    scores_again = (
+        jnp.einsum("gqhe,gkhe->ghqk", shaped[0], shaped[1], preferred_element_type=jnp.float32)
+        / score_root
+    )
+    probs_again = jnp.exp(scores_again - log_total)
+    grad_probs = jnp.einsum(
+        "gqhe,gkhe->ghqk", grad_heads, shaped[2], preferred_element_type=jnp.float32
+    )
+    grad_scores = (
+        probs_again * (grad_probs - jnp.sum(probs_again * grad_probs, axis=-1, keepdims=True))
+    ).astype(jnp.bfloat16)
+    grad_values = jnp.einsum(
+        "ghqk,gqhe->gkhe",
+        probs_again.astype(jnp.bfloat16),
+        grad_heads,
+        preferred_element_type=jnp.float32,
+    )
+    grad_queries = (
+        jnp.einsum("ghqk,gkhe->gqhe", grad_scores, shaped[1], preferred_element_type=jnp.float32)
+        / score_root
+    )
+    grad_keys = (
+        jnp.einsum("ghqk,gqhe->gkhe", grad_scores, shaped[0], preferred_element_type=jnp.float32)
+        / score_root
+    )
+    grad_qkv_rows = (
+        jnp.stack([grad_queries, grad_keys, grad_values])
+        .reshape(3, row_count, local_width)
+        .astype(jnp.bfloat16)
+    )
+    grad_qkv = jnp.einsum(
+        "td,stf->sdf", normed_one, grad_qkv_rows, preferred_element_type=jnp.float32
+    )
+    grad_normed_one = lax.psum(
+        jnp.einsum(
+            "stf,sdf->td", grad_qkv_rows, qkv_weight, preferred_element_type=jnp.float32
+        ).astype(jnp.bfloat16),
+        "tensor",
+    ).astype(jnp.float32)
+    input_back, grad_gain_attn = norm_back(grad_normed_one, unit_one, scale_one, gain_attn)
+    grad_tokens = grad_residual + input_back
+    squares = jnp.stack([jnp.sum(inputs * inputs), jnp.sum(attn * attn), jnp.sum(moe * moe)])
+    summed = lax.psum(
+        (grad_qkv, grad_out_weight, grad_gain_attn, grad_gain_moe, grad_router, squares), "expert"
+    )
+    entry_count = float(row_count * features * lax.axis_size("expert"))
+    stats = jnp.sqrt(summed[5] / entry_count)
+    return (
+        result,
+        grad_tokens,
+        summed[0],
+        summed[1],
+        summed[2],
+        summed[3],
+        summed[4],
+        grad_expert_in.astype(jnp.float32),
+        grad_expert_out.astype(jnp.float32),
+        stats,
+    )
+
+
 def solution(mesh):
     in_specs = (
         P("expert", None),
@@ -316,6 +586,7 @@
         P("expert", "tensor", None),
         P(),
     )
+    few = 2 * MOST_DENSE >= mesh.shape["expert"]
     return jax.shard_map(
-        per_device, mesh=mesh, in_specs=in_specs, out_specs=out_specs, check_vma=False
-    )
+        per_device_dense if few else per_device_slots, mesh=mesh, in_specs=in_specs, out_specs=out_specs, check_vma=False
+    )

time: 1760 us -> 525 us (0.30)
  waiting for transfers between devices: 1100 us -> 342 us
  blocking collectives: 316 us -> 55.6 us
  matrix products: 152 us -> 23.7 us
  local copies, waits for them, and re-layouts: 107 us -> 34.8 us
  other arithmetic: 51.3 us -> 26.3 us
  Pallas kernels: 0 us -> 24.3 us
    all_to_all x2 -> x0, waiting for transfers between devices: 521 us -> none  [from_experts(): lax.all_to_all(shaped_back, 'expert', split_axis=0, concat_axis=0, tiled=...]
    psum x5 -> x4, waiting for transfers between devices: 580 us -> 196 us  [the longest x1 72.8 us: per_device_dense(): lax.psum((grad_qkv, grad_out_weight, grad_gain_attn, grad_gain_moe, grad_...]
    all_to_all x2 -> x0, blocking collectives: 279 us -> none  [to_experts(): lax.all_to_all(doubled, 'expert', split_axis=0, concat_axis=0, tiled=True)]
    dot_general x39 -> x16, matrix products: 152 us -> 23.7 us  [the longest x1 5.45 us: per_device_dense(): jnp.einsum('te,de->td', grad_logits, router_weight.astype(jnp.float32), p...]
    reduce_scatter x0 -> x2, waiting for transfers between devices: none -> 94.9 us  [the longest x1 69.8 us: per_device_dense(): lax.psum_scatter(grad_out, 'expert', scatter_dimension=0, tiled=True)]
    reshape x15 -> x2, local copies, waits for them, and re-layouts: 52 us -> 2.85 us  [per_device_dense(): grad_heads.astype(jnp.bfloat16).reshape(images, LEN, heads_here, HD)]
    all_gather x0 -> x2, waiting for transfers between devices: none -> 49.1 us  [the longest x1 49.1 us: per_device_dense(): wout_all = lax.all_gather(expert_out[0], 'expert')]
    pallas_call x0 -> x1, Pallas kernels: none -> 24.3 us  [dense_experts(): pl.pallas_call(dense_experts_kernel, grid=(halves,), in_specs=[whole((row...]
  transfers between devices with their start and end apart: 7 -> 8, of which waited for: 7 -> 7; matrix products, arithmetic and copies ran while one was open for 3% -> 7% of each run, Pallas kernels for 0% -> 0%
where the time goes in v1:
time: 525 us; the launch traced here: 524 us
  waiting for transfers between devices  342 us (65%)
  blocking collectives  55.6 us (11%)
  local copies, waits for them, and re-layouts  34.8 us (7%)
  other arithmetic  26.3 us (5%)
  Pallas kernels  24.3 us (5%)
  matrix products  23.7 us (5%)
  between operations  16.2 us (3%)
    psum x1, waiting for transfers between devices, per_device_dense(): lax.psum((grad_qkv, grad_out_weight, grad_gain_attn, grad_gain_moe, grad_...  72.8 us
    reduce_scatter x1, waiting for transfers between devices, per_device_dense(): lax.psum_scatter(grad_out, 'expert', scatter_dimension=0, tiled=True)  69.8 us
    psum x1, waiting for transfers between devices, per_device_dense(): moe = lax.psum(moe_part, 'tensor')[:row_count].astype(jnp.float32)  56.3 us
    all_gather x1, waiting for transfers between devices, per_device_dense(): wout_all = lax.all_gather(expert_out[0], 'expert')  49.1 us
    psum x1, blocking collectives, per_device_dense(): lax.psum((grad_qkv, grad_out_weight, grad_gain_attn, grad_gain_moe, grad_...  37.5 us
    psum x1, waiting for transfers between devices, per_device_dense(): back_sum, gate_sum = lax.psum((back_part, gate_part), 'tensor')  34.7 us
    psum x1, waiting for transfers between devices, per_device_dense(): lax.psum(jnp.dot(head_rows, out_weight, preferred_element_type=jnp.float3...  32.4 us
    reduce_scatter x1, waiting for transfers between devices, per_device_dense(): lax.psum_scatter(grad_in, 'expert', scatter_dimension=0, tiled=True)  25.1 us
  transfers between devices with their start and end apart: 8, of which 7 were waited for; matrix products, arithmetic and copies ran while one was open for 7% of the time, Pallas kernels for 0%

profile of v1, /device:TPU:0, one launch (start us, length us, event | category | flops | bytes accessed | tf_op | source)
XLA Modules:
  0.0 524.3 jit_solution(8786658017500609874)
XLA Ops:
  8.1 1.6 fusion.11
  9.7 2.1 fusion.12
  13.8 1.1 copy.102
  15.6 1.1 copy.103
  16.7 1.6 multiply_reduce_fusion.4
  19.5 1.0 copy.105
  20.5 1.5 convert_element_type.98
  22.0 1.5 convolution_convert_fusion
  26.5 1.1 copy.111
  28.4 2.4 pad.12.dy_ref
  30.8 1.1 fusion
  31.9 32.4 %all-reduce.11.cloned.1.call-done = bf16[1182,512]{1,0:T(8,128)(2,1)} async-done(((bf16[1182,512]{1,0:T(8,128)(2,1)}), bf16[1182,512]{1,0:T(8,128)(2,1)}) %all-reduce.11.cloned.1.call-update) | async-done | bytes 1210384 | tf_op jit(solution)/shard_map/psum | solution.py:457
  64.3 2.3 multiply_reduce_fusion.3
  67.2 1.0 copy-done.10
  68.6 1.1 copy.108
  69.9 1.1 copy.148
  70.9 1.7 fusion.38
  72.6 2.4 pad.11.x_ref
  75.2 1.1 copy.110
  76.3 1.3 fusion.40
  78.4 49.1 %all-gather.5.cloned.1.call-done.wout_ref = bf16[8,256,512]{2,1,0:T(8,128)(2,1)} async-done(((bf16[1,256,512]{2,1,0:T(8,128)(2,1)}), bf16[8,256,512]{2,1,0:T(8,128)(2,1)}) %all-gather.5.cloned.1.call-update) | async-done | bytes 2097168 | tf_op jit(solution)/shard_map/all_gather | solution.py:428
  127.5 24.3 %dense_experts.1 = (bf16[1184,512]{1,0:T(8,128)(2,1)}, bf16[1184,512]{1,0:T(8,128)(2,1)}, f32[1184,4]{1,0:T(8,128)}, bf16[8,512,256]{2,1,0:T(8,128)(2,1)}, bf16[8,256,512]{2,1,0:T(8,128)(2,1)}) custom-call(bf16[1184,512]{1,0:T(8,128)(2,1)} %pad.11.x_ref, bf16[1184,512]{1,0:T(8,128)(2,1)} %pad.12.dy_ref, f32[1184,4]{1,0:T(8,128)} %pad.13.gate_ref, ...), custom_call_target="tpu_custom_call" | custom-call | tf_op jit(solution)/shard_map/dense_experts/pallas_call | solution.py:357
  151.8 18.1 %psum.80 = f32[1184,4]{1,0:T(8,128)} all-reduce(f32[1184,4]{1,0:T(8,128)} %get-tuple-element.17), channel_id=1, replica_groups=mesh['expert'=8,'tensor'=4] {'tensor'}, use_global_device_ids=true, to_apply=%region_13.14 | all-reduce | flops 4736 | bytes 37888 | tf_op jit(solution)/shard_map/psum | solution.py:475
  169.9 1.7 multiply_reduce_fusion.5
  172.1 1.1 copy.113
  173.2 34.7 %all-reduce.13.cloned.1.call-done = bf16[1184,512]{1,0:T(8,128)(2,1)} async-done(((bf16[1184,512]{1,0:T(8,128)(2,1)}), bf16[1184,512]{1,0:T(8,128)(2,1)}) %all-reduce.13.cloned.1.call-update) | async-done | bytes 1212432 | tf_op jit(solution)/shard_map/psum | solution.py:475
  207.9 5.4 %multiply_reduce_fusion.1 = (f32[512]{0:T(512)}, f32[1182]{0:T(1024)S(1)}, f32[]{:T(128)}, f32[]{:T(128)}, f32[1182,512]{1,0:T(8,128)S(1)}) fusion(bf16[1182,512]{1,0:T(8,128)(2,1)} %all-reduce.11.cloned.1.call-done, bf16[1182,512]{1,0:T(8,128)(2,1)} %param.11, f32[1182]{0:T(1024)S(1)} %add_rsqrt_fusion, f32[512]{0:T(512)S(1)} %copy-done.31, ...), kind=kOutput, calls=%fused_computation.37 | convolution fusion | flops 38139080 | bytes 6102592 | tf_op jit(solution)/shard_map/te,de->td/dot_general | solution.py:490
  214.2 1.4 copy-done.4
  216.1 1.5 reshape.101
  217.6 1.4 copy.115
  219.0 2.1 fusion.33
  224.6 1.0 fusion.43
  226.2 1.5 reshape.97
  229.5 1.5 reshape.95
  232.1 1.8 convolution_bitcast_fusion.1
  233.9 1.9 fusion.8
  237.3 1.9 fusion.46
  239.2 72.8 %all-reduce.15.cloned.1.call-done = (f32[3,512,128]{1,2,0:T(8,128)}, f32[128,512]{1,0:T(8,128)}) async-done(((f32[3,512,128]{1,2,0:T(8,128)}, f32[128,512]{1,0:T(8,128)}), (f32[3,512,128]{1,2,0:T(8,128)}, f32[128,512]{1,0:T(8,128)})) %all-reduce.15.cloned.1.call-update) | async-done | bytes 1048592 | tf_op jit(solution)/shard_map/psum | solution.py:544
  312.0 2.3 copy.129
  314.3 56.3 %all-reduce.17.cloned.1.call-done = (bf16[1184,512]{1,0:T(8,128)(2,1)}, bf16[1182,512]{1,0:T(8,128)(2,1)}) async-done(((bf16[1184,512]{1,0:T(8,128)(2,1)}, bf16[1182,512]{1,0:T(8,128)(2,1)}), (bf16[1184,512]{1,0:T(8,128)(2,1)}, bf16[1182,512]{1,0:T(8,128)(2,1)})) %all-reduce.17.cloned.1.call-update) | async-done | bytes 2422800 | tf_op jit(solution)/shard_map/psum | solution.py:476
  370.6 2.4 fusion.20
  373.0 4.6 fusion.17
  377.6 2.0 pad_maximum_fusion
  379.6 37.5 %all-reduce.3 = (f32[512]{0:T(512)}, f32[512]{0:T(512)}, f32[512,4]{0,1:T(4,128)}, f32[3]{0:T(128)S(1)}) all-reduce(f32[512]{0:T(512)S(1)} %get-tuple-element.62, f32[512]{0:T(512)S(1)} %copy-done.34, f32[512,4]{0,1:T(4,128)S(1)} %fusion.46, f32[3]{0:T(128)S(1)} %pad_maximum_fusion), channel_id=1, replica_groups=mesh['expert'=8,'tensor'=4] {'expert'}, use_global_device_ids=true, to_apply=%region_24.25 | all-reduce | flops 3075 | bytes 24600 | tf_op jit(solution)/shard_map/psum | solution.py:544
  417.7 25.1 %reduce-scatter.3.cloned.1.call-done = bf16[1,512,256]{2,1,0:T(8,128)(2,1)} async-done(((bf16[8,512,256]{2,1,0:T(8,128)(2,1)}), bf16[1,512,256]{2,1,0:T(8,128)(2,1)}) %reduce-scatter.3.cloned.1.call-update) | async-done | bytes 262160 | tf_op jit(solution)/shard_map/reduce_scatter | solution.py:477
  442.8 1.8 convert_element_type.116
  444.6 69.8 %reduce-scatter.5.cloned.1.call-done = bf16[1,256,512]{2,1,0:T(8,128)(2,1)} async-done(((bf16[8,256,512]{2,1,0:T(8,128)(2,1)}), bf16[1,256,512]{2,1,0:T(8,128)(2,1)}) %reduce-scatter.5.cloned.1.call-update) | async-done | bytes 262160 | tf_op jit(solution)/shard_map/reduce_scatter | solution.py:478
  514.3 1.8 convert_element_type.117
  (136 shorter events, 20.9 us)
Async XLA Ops:
  8.0 1.7 copy-start
  8.0 56.3 %all-reduce.11.cloned.1.call-start = ((), (), s32[]{:S(2)}) async-start(), calls=%async_computation.2 | async-start | bytes 2424832 | tf_op jit(solution)/shard_map/psum | solution.py:457
  13.1 5.2 copy-start.13
  16.7 2.1 copy-start.18
  18.8 3.2 copy-start.22
  19.5 5.5 %copy-start.28 = (s32[1182,2]{0,1:T(2,128)S(1)}, s32[1182,2]{0,1:T(2,128)}, u32[]{:S(2)}) copy-start(s32[1182,2]{0,1:T(2,128)} %param.19) | copy-start | bytes 28372
  22.0 8.8 %copy-start.16 = (bf16[1182,128]{0,1:T(8,128)(2,1)}, bf16[1182,128]{0,1:T(8,128)(2,1)S(1)}, u32[]{:S(2)}) copy-start(bf16[1182,128]{0,1:T(8,128)(2,1)S(1)} %convert_element_type.98) | copy-start | bytes 907780
  23.6 54.8 %all-gather.3.cloned.1.call-start = ((), (), s32[]{:S(2)}) async-start(), calls=%async_computation.3 | async-start | bytes 2359296 | tf_op jit(solution)/shard_map/all_gather | solution.py:427
  24.2 103.3 %all-gather.5.cloned.1.call-start = ((), (), s32[]{:S(2)}) async-start(), calls=%async_computation.4 | async-start | bytes 2359296 | tf_op jit(solution)/shard_map/all_gather | solution.py:428
  24.8 183.1 %all-reduce.13.cloned.1.call-start = ((), (), s32[]{:S(2)}) async-start(), calls=%async_computation.5 | async-start | bytes 2424832 | tf_op jit(solution)/shard_map/psum | solution.py:475
  25.7 5.2 copy-start.29
  30.8 35.8 %copy-start.30 = (f32[512]{0:T(512)S(1)}, f32[512]{0:T(512)}, u32[]{:S(2)}) copy-start(f32[512]{0:T(512)} %param.15) | copy-start | bytes 6148
  64.3 2.3 copy-start.1
  64.3 2.4 copy-start.7
  66.6 1.6 copy-start.33
  67.2 1.0 copy-start.10
  151.8 56.0 %copy-start.31 = (f32[512]{0:T(512)S(1)}, f32[512]{0:T(512)}, u32[]{:S(2)}) copy-start(f32[512]{0:T(512)} %param.15) | copy-start | bytes 6148
  171.7 140.3 %all-reduce.15.cloned.1.call-start = ((), (), s32[]{:S(2)}) async-start(), calls=%async_computation.8 | async-start | bytes 2097152 | tf_op jit(solution)/shard_map/psum | solution.py:544
  172.1 41.3 %copy-start.26 = (f32[1182]{0:T(1024)}, f32[1182]{0:T(1024)S(1)}, u32[]{:S(2)}) copy-start(f32[1182]{0:T(1024)S(1)} %get-tuple-element.70) | copy-start | bytes 14188
  207.8 5.5 %copy-start.2 = (bf16[1182,512]{1,0:T(8,128)(2,1)S(1)}, bf16[1182,512]{1,0:T(8,128)(2,1)}, u32[]{:S(2)}) copy-start(bf16[1182,512]{1,0:T(8,128)(2,1)} %param.11) | copy-start | bytes 3631108
  207.8 5.5 %copy-start.8 = (bf16[1182,512]{1,0:T(8,128)(2,1)S(1)}, bf16[1182,512]{1,0:T(8,128)(2,1)}, u32[]{:S(2)}) copy-start(bf16[1182,512]{1,0:T(8,128)(2,1)} %all-reduce.11.cloned.1.call-done) | copy-start | bytes 3631108
  207.8 5.5 %copy-start.12 = (bf16[1182,512]{1,0:T(8,128)(2,1)S(1)}, bf16[1182,512]{1,0:T(8,128)(2,1)}, u32[]{:S(2)}) copy-start(bf16[1182,512]{1,0:T(8,128)(2,1)} %param.21) | copy-start | bytes 3631108
  213.3 2.3 copy-start.23
  214.2 1.4 copy-start.4
  218.9 2.1 copy-start.19
  219.0 2.1 copy-start.25
  221.9 1.0 copy-start.14
  221.9 1.5 copy-start.15
  222.9 1.7 copy-start.5
  222.9 1.7 copy-start.17
  223.4 2.3 copy-start.20
  228.1 3.8 copy-start.21
  228.2 3.9 copy-start.3
  228.2 3.9 copy-start.32
  233.8 136.7 %all-reduce.17.cloned.1.call-start = ((), (), s32[]{:S(2)}) async-start(), calls=%async_computation.9 | async-start | bytes 4849664 | tf_op jit(solution)/shard_map/psum | solution.py:476
  235.8 1.5 copy-start.11
  235.8 1.5 copy-start.27
  235.8 207.0 %reduce-scatter.3.cloned.1.call-start = ((), (), s32[]{:S(2)}) async-start(), calls=%async_computation.6 | async-start | bytes 2359296 | tf_op jit(solution)/shard_map/reduce_scatter | solution.py:477
  236.5 277.8 %reduce-scatter.5.cloned.1.call-start = ((), (), s32[]{:S(2)}) async-start(), calls=%async_computation.7 | async-start | bytes 2359296 | tf_op jit(solution)/shard_map/reduce_scatter | solution.py:478
  239.2 133.8 %copy-start.9 = (bf16[1182,512]{1,0:T(8,128)(2,1)S(1)}, bf16[1182,512]{1,0:T(8,128)(2,1)}, u32[]{:S(2)}) copy-start(bf16[1182,512]{1,0:T(8,128)(2,1)} %all-reduce.11.cloned.1.call-done) | copy-start | bytes 3631108
  370.6 2.4 copy-start.6
  373.0 6.6 %copy-start.34 = (f32[512]{0:T(512)S(1)}, f32[512]{0:T(512)}, u32[]{:S(2)}) copy-start(f32[512]{0:T(512)} %get-tuple-element.60) | copy-start | bytes 6148
  373.0 143.1 %copy-start.24 = (f32[128,512]{1,0:T(8,128)S(1)}, f32[128,512]{1,0:T(8,128)}, u32[]{:S(2)}) copy-start(f32[128,512]{1,0:T(8,128)} %get-tuple-element.106) | copy-start | bytes 786436
Sparse Core Ops, SparseCore 0:
  23.7 40.5 all-reduce.10
  171.8 36.0 all-reduce.12
Sparse Core Ops, SparseCore 1:
  26.2 51.7 all-gather.2
  79.9 47.5 all-gather.4
  233.9 78.0 all-reduce.14
  314.4 56.1 all-reduce.16
  374.1 68.6 reduce-scatter.2
  446.4 67.9 reduce-scatter.4

commit v2 on v0

--- a/solution.py
+++ b/solution.py
@@ -1,8 +1,11 @@
+import functools
 import math
 
 import jax
 import jax.numpy as jnp
 from jax import lax
+from jax.experimental import pallas as pl
+from jax.experimental.pallas import tpu as pltpu
 from jax.sharding import PartitionSpec as P
 
 HD = 64
@@ -71,7 +74,7 @@
     return halves.astype(jnp.bfloat16).reshape(experts * capacity, width)
 
 
-def per_device(
+def per_device_slots(
     tokens,
     qkv_weight,
     out_weight,
@@ -290,6 +293,656 @@
     )
 
 
+def stage_pairs(moves):
+    return [(2 * a + x, 2 * b + x) for a, b in moves for x in range(2)]
+
+
+TO_RIGHT = stage_pairs([(0, 1), (1, 2), (2, 3)])
+TO_LEFT = stage_pairs([(1, 0), (2, 1), (3, 2)])
+ACROSS = [(i, i ^ 1) for i in range(8)]
+
+
+def mixed(a, b):
+    return (a.astype(jnp.float32) + b.astype(jnp.float32)).astype(jnp.bfloat16)
+
+
+def flipped(parts, bits, index):
+    shape = parts.shape
+    parts = parts.reshape((2,) * bits + shape[1:])
+    for b in range(bits):
+        is_set = ((index >> (bits - 1 - b)) & 1) == 1
+        parts = jnp.where(is_set, jnp.flip(parts, axis=b), parts)
+    return parts.reshape(shape)
+
+
+def flip_pairs(count, mask):
+    return [(i, i ^ mask) for i in range(count)]
+
+
+def wide(v):
+    return v.astype(jnp.float32)
+
+
+def fold(a, b, dims):
+    return lax.dot_general(a, b, (dims, ((), ())), preferred_element_type=jnp.float32)
+
+
+def rows_of(index, size):
+    return pl.ds(pl.multiple_of(index * size, 16), size)
+
+
+def image_windows(rows):
+    size = -(-(LEN + 15) // 16) * 16
+    images = rows // LEN
+    return [(min(LEN * g // 16 * 16, rows - size), LEN * g) for g in range(images)], size
+
+
+def attention_forward_kernel(
+    t_ref, x_ref, w_ref, out_ref, gain_ref,
+    send_ref, keep_ref, pass_ref, normed_ref, qkv_ref, heads_ref, lse_ref,
+):
+    rows = x_ref.shape[0]
+    quarter = rows // 4
+    for c in range(4):
+        part = pl.ds(c * quarter, quarter)
+        x = wide(x_ref[part, :])
+        scaling = lax.rsqrt(jnp.mean(x * x, axis=1, keepdims=True) + EPSILON)
+        normed = (x * scaling * gain_ref[...]).astype(jnp.bfloat16)
+        normed_ref[part, :] = normed
+        for s in range(3):
+            qkv_ref[s, part, :] = fold(normed, w_ref[s], ((1,), (0,))).astype(jnp.bfloat16)
+    width = heads_ref.shape[1]
+    heads_ref[...] = jnp.zeros_like(heads_ref)
+    lse_ref[...] = jnp.zeros_like(lse_ref)
+    windows, size = image_windows(rows)
+    lane = lax.broadcasted_iota(jnp.int32, (1, width), 1)
+    spot = lax.broadcasted_iota(jnp.int32, (size, 1), 0)
+    key_spot = lax.broadcasted_iota(jnp.int32, (1, size), 1)
+    for start, first in windows:
+        part = pl.ds(start, size)
+        low = first - start
+        q = qkv_ref[0, part, :]
+        k = qkv_ref[1, part, :]
+        v = qkv_ref[2, part, :]
+        inside = (spot >= low) & (spot < low + LEN)
+        key_inside = (key_spot >= low) & (key_spot < low + LEN)
+        total = None
+        for h in range(width // HD):
+            own = (lane >= h * HD) & (lane < (h + 1) * HD)
+            scores = fold(q, jnp.where(own, k, 0), ((1,), (1,))) * (1.0 / math.sqrt(HD))
+            scores = jnp.where(key_inside, scores, -1e30)
+            peak = jnp.max(scores, axis=1, keepdims=True)
+            weights = jnp.exp(scores - peak)
+            weight_total = jnp.sum(weights, axis=1, keepdims=True)
+            probs = (weights / weight_total).astype(jnp.bfloat16)
+            lse = peak + jnp.log(weight_total)
+            lse_ref[h, part, :] = jnp.where(inside, lse, lse_ref[h, part, :])
+            rows_out = fold(probs, jnp.where(own, v, 0), ((1,), (0,)))
+            total = rows_out if total is None else total + rows_out
+        heads_ref[part, :] = jnp.where(inside, total.astype(jnp.bfloat16), heads_ref[part, :])
+    for k in range(4):
+        part = rows_of(t_ref[0] ^ k, quarter)
+        attn = fold(heads_ref[part, :], out_ref[...], ((1,), (0,))).astype(jnp.bfloat16)
+        if k % 2:
+            send_ref[k // 2] = attn
+        elif k == 0:
+            keep_ref[...] = attn
+        else:
+            pass_ref[...] = attn
+
+
+def attention_backward_kernel(
+    t_ref, g0_ref, g1_ref, g2_ref, g3_ref, w_ref, out_ref,
+    normed_ref, qkv_ref, heads_ref, lse_ref,
+    send_ref, keep_ref, pass_ref, wsend_ref, wkeep_ref, gain_ref,
+    grad_ref, ghead_ref, grow_ref,
+):
+    rows, width = heads_ref.shape
+    quarter = rows // 4
+    for k, ref in enumerate((g0_ref, g1_ref, g2_ref, g3_ref)):
+        grad_ref[rows_of(t_ref[0] ^ k, quarter), :] = ref[...]
+    ghead_ref[...] = fold(grad_ref[...], out_ref[...], ((1,), (1,))).astype(jnp.bfloat16)
+    grow_ref[...] = jnp.zeros_like(grow_ref)
+    windows, size = image_windows(rows)
+    lane = lax.broadcasted_iota(jnp.int32, (1, width), 1)
+    spot = lax.broadcasted_iota(jnp.int32, (size, 1), 0)
+    key_spot = lax.broadcasted_iota(jnp.int32, (1, size), 1)
+    scale = 1.0 / math.sqrt(HD)
+    for start, first in windows:
+        part = pl.ds(start, size)
+        low = first - start
+        q = qkv_ref[0, part, :]
+        k = qkv_ref[1, part, :]
+        v = qkv_ref[2, part, :]
+        gh = ghead_ref[part, :]
+        inside = (spot >= low) & (spot < low + LEN)
+        key_inside = (key_spot >= low) & (key_spot < low + LEN)
+        both = inside & key_inside
+        sums = [0.0, 0.0, 0.0]
+        for h in range(width // HD):
+            own = (lane >= h * HD) & (lane < (h + 1) * HD)
+            k_own = jnp.where(own, k, 0)
+            scores = fold(q, k_own, ((1,), (1,))) * scale
+            probs = jnp.where(both, jnp.exp(jnp.where(both, scores - lse_ref[h, part, :], 0.0)), 0.0)
+            gprobs = fold(gh, jnp.where(own, v, 0), ((1,), (1,)))
+            inner = jnp.sum(probs * gprobs, axis=1, keepdims=True)
+            gscores = (probs * (gprobs - inner)).astype(jnp.bfloat16)
+            sums[0] = sums[0] + fold(gscores, k_own, ((1,), (0,)))
+            sums[1] = sums[1] + fold(gscores, jnp.where(own, q, 0), ((0,), (0,)))
+            sums[2] = sums[2] + fold(
+                probs.astype(jnp.bfloat16), jnp.where(own, gh, 0), ((0,), (0,))
+            )
+        grow_ref[0, part, :] += sums[0] * scale
+        grow_ref[1, part, :] += sums[1] * scale
+        grow_ref[2, part, :] += sums[2]
+    gain = None
+    for s in range(4):
+        if s < 3:
+            grow = grow_ref[s].astype(jnp.bfloat16)
+            made = fold(normed_ref[...], grow, ((0,), (0,)))
+            seen = jnp.sum(made * wide(w_ref[s]), axis=1, keepdims=True)
+            gain = seen if gain is None else gain + seen
+        else:
+            made = fold(grad_ref[...], heads_ref[...], ((0,), (0,)))
+        made = made.astype(jnp.bfloat16)
+
+        @pl.when(t_ref[1] == s // 2)
+        def _():
+            wkeep_ref[s % 2] = made
+
+        @pl.when(t_ref[1] != s // 2)
+        def _():
+            wsend_ref[s % 2] = made
+
+    gain_ref[...] = gain
+    for k in range(4):
+        part = rows_of(t_ref[0] ^ k, quarter)
+        back = None
+        for s in range(3):
+            one = fold(grow_ref[s, part, :].astype(jnp.bfloat16), w_ref[s], ((1,), (1,)))
+            back = one if back is None else back + one
+        back = back.astype(jnp.bfloat16)
+        if k % 2:
+            send_ref[k // 2] = back
+        elif k == 0:
+            keep_ref[...] = back
+        else:
+            pass_ref[...] = back
+
+
+def norm_two_kernel(
+    x_ref, keep_ref, got_ref, other_ref, gain_ref, residual_ref, normed_ref, square_ref
+):
+    attn = (wide(keep_ref[...]) + wide(got_ref[0])) + wide(other_ref[...])
+    x = wide(x_ref[...])
+    residual = x + attn
+    residual_ref[...] = residual
+    scaling = lax.rsqrt(jnp.mean(residual * residual, axis=1, keepdims=True) + EPSILON)
+    normed_ref[...] = (residual * scaling * gain_ref[...]).astype(jnp.bfloat16)
+    square_ref[0:1, :] = jnp.sum(x * x, axis=0, keepdims=True)
+    square_ref[1:2, :] = jnp.sum(attn * attn, axis=0, keepdims=True)
+
+
+def norm_one_back_kernel(
+    x_ref, keep_ref, got_ref, other_ref, before_ref, gain_ref, grad_ref
+):
+    incoming = (wide(keep_ref[...]) + wide(got_ref[0])) + wide(other_ref[...])
+    x = wide(x_ref[...])
+    scaling = lax.rsqrt(jnp.mean(x * x, axis=1, keepdims=True) + EPSILON)
+    unit = x * scaling
+    inner = incoming * gain_ref[...]
+    back = scaling * (inner - unit * jnp.mean(inner * unit, axis=1, keepdims=True))
+    grad_ref[...] = (before_ref[...] + back).astype(jnp.bfloat16)
+
+
+def pair_gates(normed, router, code):
+    rows = normed.shape[0]
+    logits = fold(normed, router, ((1,), (0,)))
+    lane = lax.broadcasted_iota(jnp.int32, (rows, router.shape[1]), 1)
+    lead = wide(lane == (code & 31))
+    trail = wide(lane == ((code >> 5) & 31))
+    one = jnp.sum(lead * logits, axis=1, keepdims=True)
+    two = jnp.sum(trail * logits, axis=1, keepdims=True)
+    peak = jnp.maximum(one, two)
+    one = jnp.exp(one - peak)
+    two = jnp.exp(two - peak)
+    both = one + two
+    kept_one = wide((code >> 10) & 1)
+    kept_two = wide((code >> 11) & 1)
+    return lead, trail, one / both, two / both, kept_one, kept_two
+
+
+def norm_two_back_kernel(
+    keep_ref, got_ref, other_ref, residual_ref, dy_ref, code_ref, gain_ref, router_ref, flat_ref,
+    grad_ref, low_ref, small_ref,
+):
+    features = residual_ref.shape[1]
+    experts = flat_ref.shape[0]
+    total = (wide(keep_ref[...]) + wide(got_ref[0])) + wide(other_ref[...])
+    residual = residual_ref[...]
+    scaling = lax.rsqrt(jnp.mean(residual * residual, axis=1, keepdims=True) + EPSILON)
+    unit = residual * scaling
+    normed = (unit * gain_ref[...]).astype(jnp.bfloat16)
+    lead, trail, one, two, kept_one, kept_two = pair_gates(normed, router_ref[...], code_ref[...])
+    seen = total[:, features:]
+    seen = seen + pltpu.roll(seen, 64, axis=1)
+    back_one = kept_one * jnp.sum(lead * seen, axis=1, keepdims=True)
+    back_two = kept_two * jnp.sum(trail * seen, axis=1, keepdims=True)
+    mean = one * back_one + two * back_two
+    choice = lead * (one * (back_one - mean)) + trail * (two * (back_two - mean))
+    incoming = total[:, :features]
+    for e in range(experts):
+        column = choice[:, e : e + 1]
+        incoming = incoming + column * flat_ref[e : e + 1, :]
+        small_ref[1 + e : 2 + e, :] = jnp.sum(column * wide(normed), axis=0, keepdims=True)
+    inner = incoming * gain_ref[...]
+    small_ref[0:1, :] = jnp.sum(incoming * unit, axis=0, keepdims=True)
+    back = scaling * (inner - unit * jnp.mean(inner * unit, axis=1, keepdims=True))
+    grad = wide(dy_ref[...]) + back
+    grad_ref[...] = grad
+    low_ref[...] = grad.astype(jnp.bfloat16)
+
+
+def dense_experts_kernel(
+    which_ref, x0_ref, x1_ref, x2_ref, x3_ref, dy_ref, code_ref, router_ref, *refs, last
+):
+    count = 4
+    w_refs, refs = refs[:count], refs[count:]
+    if last:
+        before, refs = refs[:3], refs[3:]
+        msend_ref, mkeep_ref, mpass_ref, dsend_ref, dkeep_ref, dpass_ref = refs[:6]
+        g_refs, refs = refs[6 : 6 + count], refs[6 + count :]
+        moe_acc, dx_acc, gg_acc = refs[:3]
+        refs = refs[3:]
+    else:
+        moe_acc, dx_acc, gg_acc = refs[:3]
+        g_refs, refs = refs[3 : 3 + count], refs[3 + count :]
+    x_ref, gate_ref, w_now, gact_ref, gpre_ref, g_now = refs
+    step = pl.program_id(0)
+    chosen = which_ref[step]
+    rows, features = dy_ref.shape
+    quarter = rows // 4
+
+    @pl.when(step == 0)
+    def _():
+        moe_acc[...] = jnp.zeros_like(moe_acc)
+        dx_acc[...] = jnp.zeros_like(dx_acc)
+        gg_acc[...] = jnp.zeros_like(gg_acc)
+        for k, ref in enumerate((x0_ref, x1_ref, x2_ref, x3_ref)):
+            x_ref[rows_of(which_ref[count] ^ k, quarter), :] = ref[...]
+        for c in range(4):
+            part = pl.ds(c * quarter, quarter)
+            lead, trail, one, two, kept_one, kept_two = pair_gates(
+                x_ref[part, :], router_ref[...], code_ref[part, :]
+            )
+            gate_ref[part, :] = lead * (one * kept_one) + trail * (two * kept_two)
+
+    for k in range(count):
+
+        @pl.when(step == k)
+        def _():
+            w_now[...] = w_refs[k][...]
+
+    hidden = gact_ref.shape[1]
+    pieces = [pl.ds(i, hidden) for i in range(0, features, hidden)]
+    wout = w_now[1]
+    for c in range(4):
+        part = pl.ds(c * quarter, quarter)
+        pre = fold(x_ref[part, pieces[0]], w_now[0, :, pieces[0]], ((1,), (0,)))
+        for piece in pieces[1:]:
+            pre = pre + fold(x_ref[part, piece], w_now[0, :, piece], ((1,), (0,)))
+        back = fold(dy_ref[part, :], wout, ((1,), (1,)))
+        half = 0.5 + 0.5 * lax.erf(pre * math.sqrt(0.5))
+        act = pre * half
+        slope = half + pre * (jnp.exp(pre * pre * -0.5) * (1.0 / math.sqrt(2.0 * math.pi)))
+        lane = lax.broadcasted_iota(jnp.int32, (quarter, 128), 1)
+        mine = lane == chosen
+        gate = jnp.sum(jnp.where(mine, gate_ref[part, :], 0.0), axis=1, keepdims=True)
+        act = wide(act.astype(jnp.bfloat16))
+        seen = jnp.sum(act * back, axis=1, keepdims=True)
+        gg_acc[part, :] = gg_acc[part, :] + jnp.where(mine, seen, 0.0)
+        gact_ref[part, :] = (gate * act).astype(jnp.bfloat16)
+        gpre_ref[part, :] = (gate * back * slope).astype(jnp.bfloat16)
+    gact = gact_ref[...]
+    gpre = gpre_ref[...]
+    moe_acc[...] += fold(gact, wout, ((1,), (0,)))
+    for piece in pieces:
+        dx_acc[:, piece] += fold(gpre, w_now[0, :, piece], ((1,), (1,)))
+        g_now[0, :, piece] = fold(x_ref[:, piece], gpre, ((0,), (0,))).astype(jnp.bfloat16)
+    g_now[1] = fold(gact, dy_ref[...], ((0,), (0,))).astype(jnp.bfloat16)
+    for k in range(count):
+
+        @pl.when(step == k)
+        def _():
+            g_refs[k][...] = g_now[...]
+
+    if not last:
+        return
+
+    @pl.when(step == count - 1)
+    def _():
+        moe_in, dx_in, gg_in = before
+        for k in range(4):
+            part = rows_of(which_ref[count] ^ k, quarter)
+            moe = (moe_acc[part, :] + moe_in[part, :]).astype(jnp.bfloat16)
+            dx = (dx_acc[part, :] + dx_in[part, :]).astype(jnp.bfloat16)
+            seen = gg_acc[part, :] + gg_in[part, :]
+            high = wide(seen.astype(jnp.bfloat16))
+            seen = (high + pltpu.roll(seen - high, 64, axis=1)).astype(jnp.bfloat16)
+            if k % 2:
+                msend_ref[k // 2] = moe
+                dsend_ref[k // 2, :, :features] = dx
+                dsend_ref[k // 2, :, features:] = seen
+            else:
+                (mpass_ref if k else mkeep_ref)[...] = moe
+                into = dpass_ref if k else dkeep_ref
+                into[:, :features] = dx
+                into[:, features:] = seen
+
+
+def one_step(kernel, scalars, args, outs, scratch=(), grid=1):
+    whole = lambda v: pl.BlockSpec(v.shape, lambda j, w, n=len(v.shape): (0,) * n)
+    return pl.pallas_call(
+        kernel,
+        grid_spec=pltpu.PrefetchScalarGridSpec(
+            num_scalar_prefetch=1,
+            grid=(grid,),
+            in_specs=[whole(v) for v in args],
+            out_specs=[whole(v) for v in outs],
+            scratch_shapes=[pltpu.VMEM(shape, dtype) for shape, dtype in scratch],
+        ),
+        out_shape=outs,
+    )(scalars, *args)
+
+
+def drop_first(kernel):
+    return lambda scalars, *refs: kernel(*refs)
+
+
+def array_of(shape, dtype=jnp.bfloat16):
+    return jax.ShapeDtypeStruct(shape, dtype)
+
+
+def after(values, *tokens):
+    return lax.optimization_barrier((values, tokens))[0]
+
+
+def flip_core(v):
+    return lax.ppermute(v, "tensor", flip_pairs(4, 1))
+
+
+def flip_row(v):
+    return lax.ppermute(v, "tensor", flip_pairs(4, 2))
+
+
+def over(v, pairs):
+    return lax.ppermute(v, "expert", pairs)
+
+
+def pair_codes(expert_ids, ranking, experts, capacity):
+    iota = jnp.arange(experts, dtype=jnp.int32)[None, :]
+    leading = (expert_ids[:, 0:1] == iota).astype(jnp.bfloat16)
+    trailing = (expert_ids[:, 1:2] == iota).astype(jnp.bfloat16)
+    earlier = (ranking[None, :] < ranking[:, None]).astype(jnp.bfloat16)
+    before = jnp.dot(
+        earlier, jnp.concatenate([leading, trailing], axis=1), preferred_element_type=jnp.float32
+    )
+    lead_place = jnp.sum(before[:, :experts] * wide(leading), axis=1)
+    totals = jnp.sum(wide(leading), axis=0)
+    trail_place = jnp.sum((before[:, experts:] + totals) * wide(trailing), axis=1)
+    bits = lambda place: (place < capacity).astype(jnp.int32)
+    code = expert_ids[:, 0] + 32 * expert_ids[:, 1]
+    return (code + 1024 * bits(lead_place) + 2048 * bits(trail_place))[:, None]
+
+
+def dense_body(
+    tokens,
+    qkv_weight,
+    out_weight,
+    gain_attn,
+    gain_moe,
+    router_weight,
+    expert_in,
+    expert_out,
+    expert_ids,
+    priority,
+    cotangent,
+):
+    row_count, features = tokens.shape
+    width = qkv_weight.shape[2]
+    hidden = expert_in.shape[2]
+    experts = router_weight.shape[1]
+    capacity = max(2, 5 * row_count // (2 * experts))
+    padded = -(-row_count // 64) * 64
+    quarter = padded // 4
+    f32 = jnp.float32
+    t = lax.axis_index("tensor").astype(jnp.int32)
+    d = lax.axis_index("expert").astype(jnp.int32)
+    place = d // 2
+    pad = lambda v: jnp.pad(v, ((0, padded - row_count), (0, 0)))
+    mine = lambda v: lax.dynamic_slice_in_dim(v, t * quarter, quarter, 0)
+    w_in = jnp.concatenate(jnp.split(expert_in[0], features // hidden), axis=1)
+    own = jnp.stack([w_in, expert_out[0]])
+    right = over(own, TO_RIGHT)
+    left = over(own, TO_LEFT)
+    cross_own = over(own, ACROSS)
+    x_all = pad(tokens)
+    dy_all = pad(cotangent)
+    gain_one = gain_attn[None]
+    gain_two = gain_moe[None]
+    spots = jnp.stack([t, d % 2])
+    part = array_of((quarter, features))
+    parts = array_of((2, quarter, features))
+    send, keep, passed, normed_one, qkv, head_rows, lse = one_step(
+        attention_forward_kernel,
+        spots,
+        [x_all, qkv_weight, out_weight, gain_one],
+        [
+            parts,
+            part,
+            part,
+            array_of((padded, features)),
+            array_of((3, padded, width)),
+            array_of((padded, width)),
+            array_of((width // HD, padded, 1), f32),
+        ],
+    )
+    got = flip_core(send)
+    right, left = after((right, left), send)
+    near = jnp.where(place >= 1, right, left)
+    passed = mixed(passed, got[1])
+    other = flip_row(passed)
+    right_two = over(right, stage_pairs([(1, 2), (2, 3)]))
+    left_two = over(left, stage_pairs([(1, 0), (2, 1)]))
+    cross_near = over(near, ACROSS)
+    right_two, left_two = after((right_two, left_two), passed)
+    middle = jnp.where(place >= 2, right_two, left_two)
+    end = over(middle, stage_pairs([(2, 3), (1, 0)]))
+    cross_middle = over(middle, ACROSS)
+    other = after(other, middle)
+    x_here = mine(x_all)
+    dy_here = mine(dy_all)
+    residual, normed_two, squares = one_step(
+        drop_first(norm_two_kernel),
+        spots,
+        [x_here, keep, got, other, gain_two],
+        [array_of((quarter, features), f32), part, array_of((2, features), f32)],
+    )
+    row_two = flip_row(normed_two)
+    core_two = flip_core(normed_two)
+    end, left = after((end, left), normed_two)
+    far = jnp.where((place == 1) | (place == 2), left, end)
+    cross_far = over(far, ACROSS)
+    row_two = after(row_two, far)
+    quarters = [normed_two, core_two, row_two, flip_core(row_two)]
+    codes = pad(pair_codes(expert_ids, priority[0], experts, capacity))
+    router_wide = jnp.pad(router_weight, ((0, 0), (0, 128 - experts)))
+    near_place = jnp.where(place >= 1, place - 1, 1)
+    far_place = jnp.where(place == 1, 2, jnp.where(place == 3, 0, 3))
+    which_near = jnp.stack([near_place, place ^ 2, near_place, place ^ 2, t])
+    which_far = jnp.stack([place, far_place, place, far_place, t])
+    one = array_of((2, hidden, features))
+    plus = (quarter, features + 128)
+    sums = [
+        array_of((padded, features), f32),
+        array_of((padded, features), f32),
+        array_of((padded, 128), f32),
+    ]
+    scratch = [
+        ((padded, features), jnp.bfloat16),
+        ((padded, 128), f32),
+        (one.shape, jnp.bfloat16),
+        ((padded, hidden), jnp.bfloat16),
+        ((padded, hidden), jnp.bfloat16),
+        (one.shape, jnp.bfloat16),
+    ]
+    shared = quarters + [dy_all, codes, router_wide]
+    early = one_step(
+        functools.partial(dense_experts_kernel, last=False),
+        which_near,
+        shared + [near, middle, cross_near, cross_middle],
+        sums + [one] * 4,
+        scratch=scratch,
+        grid=4,
+    )
+    near, middle, cross_near, cross_middle = early[3:]
+    cross_middle = over(cross_middle, ACROSS)
+    cross_near = over(cross_near, ACROSS)
+    late = one_step(
+        functools.partial(dense_experts_kernel, last=True),
+        which_far,
+        shared + after([own, far, cross_own, cross_far], early[2]) + list(early[:3]),
+        [parts, part, part, array_of((2,) + plus), array_of(plus), array_of(plus)] + [one] * 4,
+        scratch=[(v.shape, f32) for v in sums] + scratch,
+        grid=4,
+    )
+    own, far, cross_own, cross_far = late[6:]
+    msend, mkeep, mpass, dsend, dkeep, dpass = late[:6]
+    got = flip_core(dsend)
+    dpass = mixed(dpass, got[1])
+    other = flip_row(dpass)
+    cross_far, cross_own = after((cross_far, cross_own), dpass)
+    cross_far = over(cross_far, ACROSS)
+    cross_own = over(cross_own, ACROSS)
+    cross_middle, cross_near = after((cross_middle, cross_near), dpass)
+    middle = mixed(middle, cross_middle)
+    near = mixed(near, cross_near)
+    g_middle = over(middle, flip_pairs(8, 4))
+    grad_residual, grad_attn, small_two = one_step(
+        drop_first(norm_two_back_kernel),
+        spots,
+        [
+            dkeep, got, other, residual, dy_here, mine(codes), gain_two, router_wide,
+            wide(router_weight).T,
+        ],
+        [
+            array_of((quarter, features), f32),
+            part,
+            array_of((1 + experts, features), f32),
+        ],
+    )
+    row_two = flip_row(grad_attn)
+    core_two = flip_core(grad_attn)
+    far = mixed(far, after(cross_far, grad_attn))
+    turn = lambda by: [(i, (i + 2 * by) % 8) for i in range(8)]
+    g_right = over(jnp.where(place == 0, near, far), turn(1))
+    g_left = over(jnp.where(place == 0, far, near), turn(-1))
+    mgot = flip_core(after(msend, grad_attn))
+    mpass = mixed(mpass, mgot[1])
+    mother = flip_row(mpass)
+    row_two = after(row_two, far, mpass)
+    both_two = flip_core(row_two)
+    send, keep, passed, wsend, wkeep, gain_column = one_step(
+        attention_backward_kernel,
+        spots,
+        [grad_attn, core_two, row_two, both_two]
+        + [qkv_weight, out_weight, normed_one, qkv, head_rows, lse],
+        [
+            parts,
+            part,
+            part,
+            array_of((2, features, width)),
+            array_of((2, features, width)),
+            array_of((features, 1), f32),
+        ],
+        scratch=[
+            ((padded, features), jnp.bfloat16),
+            ((padded, width), jnp.bfloat16),
+            ((3, padded, width), f32),
+        ],
+    )
+    got = flip_core(send)
+    wgot = over(wsend, flip_pairs(8, 1))
+    passed = mixed(passed, got[1])
+    other = flip_row(passed)
+    mother, g_middle, g_right, g_left = after((mother, g_middle, g_right, g_left), passed)
+    moe = (wide(mkeep) + wide(mgot[0])) + wide(mother)
+    result = (residual + moe).astype(jnp.bfloat16)
+    small = jnp.concatenate(
+        [
+            gain_column[:, 0][None] / gain_one,
+            small_two,
+            squares,
+            jnp.sum(moe * moe, axis=0, keepdims=True),
+        ]
+    )
+    small = small + flip_core(small)
+    s_got = flip_row(small)
+    grads = mixed(wkeep, after(wgot, small))
+    wgot = over(grads, flip_pairs(8, 2))
+    small = small + after(s_got, grads)
+    s_got = over(small, flip_pairs(8, 1))
+    grad_tokens = one_step(
+        drop_first(norm_one_back_kernel),
+        spots,
+        [x_here, keep, got, after(other, small), grad_residual, gain_one],
+        [part],
+    )[0]
+    grad_row = flip_row(grad_tokens)
+    grad_core = flip_core(grad_tokens)
+    result_row = flip_row(after(result, grad_tokens))
+    result_core = flip_core(after(result, grad_tokens))
+    grads = mixed(grads, after(wgot, grad_tokens))
+    wgot = over(grads, flip_pairs(8, 4))
+    small = small + after(s_got, grads)
+    s_got = over(small, flip_pairs(8, 2))
+    grad_row = after(grad_row, small)
+    ordered = lambda four: flipped(jnp.stack(four), 2, t).reshape(padded, features)[:row_count]
+    grad_tokens = ordered([grad_tokens, grad_core, grad_row, flip_core(grad_row)])
+    small = small + after(s_got, grad_tokens)
+    s_got = over(small, flip_pairs(8, 4))
+    grads = mixed(grads, after(wgot, grad_tokens))
+    wgot = over(grads, flip_pairs(8, 1))
+    result_row = after(result_row, grads)
+    result = ordered([result, result_core, result_row, flip_core(result_row)])
+    grad_expert = (wide(own) + wide(after(cross_own, grads))) + (
+        wide(g_middle) + (wide(g_right) + wide(g_left))
+    )
+    small = small + after(s_got, result)
+    wgot = after(wgot, result)
+    weight_grads = flipped(jnp.stack([grads, wgot]), 1, d % 2).reshape(4, features, width)
+    weight_grads = wide(weight_grads)
+    grad_in = jnp.concatenate(jnp.split(grad_expert[0], features // hidden, axis=1), axis=0)
+    entry_count = float(row_count * features * lax.axis_size("expert"))
+    stats = jnp.sqrt(jnp.sum(small[2 + experts :], axis=1) / entry_count)
+    return (
+        result,
+        wide(grad_tokens),
+        weight_grads[:3],
+        weight_grads[3].T,
+        small[0],
+        small[1],
+        small[2 : 2 + experts].T,
+        grad_in[None],
+        grad_expert[1][None],
+        stats,
+    )
+
+
+def per_device_dense(*args):
+    return dense_body(*args)
+
+
 def solution(mesh):
     in_specs = (
         P("expert", None),
@@ -316,6 +969,7 @@
         P("expert", "tensor", None),
         P(),
     )
+    few = mesh.shape["expert"] == 8 and mesh.shape["tensor"] == 4
     return jax.shard_map(
-        per_device, mesh=mesh, in_specs=in_specs, out_specs=out_specs, check_vma=False
-    )
+        per_device_dense if few else per_device_slots, mesh=mesh, in_specs=in_specs, out_specs=out_specs, check_vma=False
+    )

time: 1760 us -> 283 us (0.16)
  waiting for transfers between devices: 1100 us -> 111 us
  blocking collectives: 316 us -> 0 us
  matrix products: 152 us -> 1.09 us
  local copies, waits for them, and re-layouts: 107 us -> 17.7 us
  Pallas kernels: 0 us -> 71.5 us
  starting transfers between devices: 11.4 us -> 50.2 us
  other arithmetic: 51.3 us -> 29.2 us
    psum x5 -> x0, waiting for transfers between devices: 580 us -> none  [the longest x2 425 us: tensor_total(): return lax.psum(summand, 'tensor')]
    all_to_all x2 -> x0, waiting for transfers between devices: 521 us -> none  [from_experts(): lax.all_to_all(shaped_back, 'expert', split_axis=0, concat_axis=0, tiled=...]
    all_to_all x2 -> x0, blocking collectives: 279 us -> none  [to_experts(): lax.all_to_all(doubled, 'expert', split_axis=0, concat_axis=0, tiled=True)]
    dot_general x39 -> x1, matrix products: 152 us -> 1.09 us  [pair_codes(): jnp.dot(earlier, jnp.concatenate([leading, trailing], axis=1), preferred_...]
    ppermute x0 -> x45, waiting for transfers between devices: none -> 111 us  [the longest x23 93.5 us: over(): return lax.ppermute(v, 'expert', pairs)]
    pallas_call x0 -> x7, Pallas kernels: none -> 71.5 us  [one_step(): pl.pallas_call(kernel, grid_spec=pltpu.PrefetchScalarGridSpec(num_scalar_...]
    reshape x15 -> x0, local copies, waits for them, and re-layouts: 52 us -> none  [the longest x2 23.9 us: from_experts(): shaped_back = rows_back.reshape(2 * experts, capacity, rows_back.shape[1])]
    ppermute x0 -> x45, starting transfers between devices: none -> 50.2 us  [the longest x23 41.6 us: over(): return lax.ppermute(v, 'expert', pairs)]
  transfers between devices with their start and end apart: 7 -> 45, of which waited for: 7 -> 18; matrix products, arithmetic and copies ran while one was open for 3% -> 14% of each run, Pallas kernels for 0% -> 13%
where the time goes in v2:
time: 283 us; the launch traced here: 282 us
  waiting for transfers between devices  111 us (39%)
  Pallas kernels  71.5 us (25%)
  starting transfers between devices  50.2 us (18%)
  other arithmetic  29.2 us (10%)
  local copies, waits for them, and re-layouts  17.7 us (6%)
    ppermute x23, waiting for transfers between devices, over(): return lax.ppermute(v, 'expert', pairs)  93.5 us
    pallas_call x7, Pallas kernels, one_step(): pl.pallas_call(kernel, grid_spec=pltpu.PrefetchScalarGridSpec(num_scalar_...  71.5 us
    ppermute x23, starting transfers between devices, over(): return lax.ppermute(v, 'expert', pairs)  41.6 us
    ppermute x9, waiting for transfers between devices, flip_row(): return lax.ppermute(v, 'tensor', flip_pairs(4, 2))  11.6 us
    ppermute x9, starting transfers between devices, flip_row(): return lax.ppermute(v, 'tensor', flip_pairs(4, 2))  8.17 us
    convert_element_type x8, other arithmetic, mixed(): return (a.astype(jnp.float32) + b.astype(jnp.float32)).astype(jnp.bfloat16)  6.67 us
  transfers between devices with their start and end apart: 45, of which 18 were waited for; matrix products, arithmetic and copies ran while one was open for 14% of the time, Pallas kernels for 13%

profile of v2, /device:TPU:0, one launch (start us, length us, event | category | flops | bytes accessed | tf_op | source)
XLA Modules:
  0.0 281.6 jit_solution(12417895435934740342)
XLA Ops:
  2.8 3.0 %collective-permute-start.10 = (bf16[2,256,512]{2,1,0:T(8,128)(2,1)S(1)}, bf16[2,256,512]{2,1,0:T(8,128)(2,1)}, u32[]{:S(2)}, u32[]{:S(2)}) collective-permute-start(bf16[2,256,512]{2,1,0:T(8,128)(2,1)S(1)} %pad_maximum_fusion.2.refs_0_), channel_id=1, source_target_pairs={{0,4},{4,0},{8,12},{12,8},{16,20},{20,16},{24,28},{28,24},{1,5},{5... | collective-permute-start | bytes 1572872 | tf_op jit(solution)/shard_map/ppermute | solution.py:679
  5.8 1.3 collective-permute-start.3
  7.1 4.6 %collective-permute-start.2 = (bf16[2,256,512]{2,1,0:T(8,128)(2,1)S(1)}, bf16[2,256,512]{2,1,0:T(8,128)(2,1)S(1)}, u32[]{:S(2)}, u32[]{:S(2)}) collective-permute-start(bf16[2,256,512]{2,1,0:T(8,128)(2,1)S(1)} %pad_maximum_fusion.2.refs_0_), channel_id=1, source_target_pairs={{0,8},{4,12},{8,16},{12,20},{16,24},{20,28},{1,9},{5,13},{9,17},{1... | collective-permute-start | bytes 1572872 | tf_op jit(solution)/shard_map/ppermute | solution.py:679
  13.5 7.2 %shard_map.186 = (bf16[2,304,512]{2,1,0:T(8,128)(2,1)}, bf16[304,512]{1,0:T(8,128)(2,1)}, bf16[304,512]{1,0:T(8,128)(2,1)}, bf16[1216,512]{1,0:T(8,128)(2,1)}, b...) custom-call(s32[2]{0:T(128)} %pad_add_fusion.t_ref.scalars, ...), custom_call_target="tpu_custom_call" | custom-call | tf_op jit(solution)/shard_map/pallas_call | solution.py:645
  22.6 1.5 collective-permute-start.4
  24.1 1.3 collective-permute-start.5
  26.1 1.2 fusion.8
  27.4 1.6 collective-permute-start.1
  28.9 13.9 %collective-permute-done.5 = bf16[2,256,512]{2,1,0:T(8,128)(2,1)} collective-permute-done((bf16[2,256,512]{2,1,0:T(8,128)(2,1)S(1)}, bf16[2,256,512]{2,1,0:T(8,128)(2,1)}, u32[]{:S(2)}, u32[]{:S(2)}) %collective-permute-start.5) | collective-permute-done | bytes 524320 | tf_op jit(solution)/shard_map/ppermute | solution.py:679
  42.8 1.9 broadcast_select_fusion.4.refs_1_
  44.7 1.5 collective-permute-start.8
  48.4 3.4 %shard_map.187 = (f32[304,512]{1,0:T(8,128)}, bf16[304,512]{1,0:T(8,128)(2,1)}, f32[2,512]{1,0:T(2,128)}) custom-call(s32[2]{0:T(128)} %pad_add_fusion.t_ref.scalars, bf16[304,512]{1,0:T(8,128)(2,1)} %constant_dynamic-slice_fusion.2.refs_0_, bf16[304,512]{1,0:T(8,128)(2,1)} %get-tuple-element.82.refs_1_, bf16[2,304,512]{2,1,0:T(8,128)(2,1)} %copy-done.7, ...), custom_call_target="tpu_custom_call" | custom-call | tf_op jit(solution)/shard_map/pallas_call | solution.py:645
  51.7 1.5 collective-permute-start.7
  55.3 4.5 %collective-permute-done.8 = bf16[2,256,512]{2,1,0:T(8,128)(2,1)} collective-permute-done((bf16[2,256,512]{2,1,0:T(8,128)(2,1)}, bf16[2,256,512]{2,1,0:T(8,128)(2,1)}, u32[]{:S(2)}, u32[]{:S(2)}) %collective-permute-start.8) | collective-permute-done | bytes 524320 | tf_op jit(solution)/shard_map/ppermute | solution.py:679
  60.3 1.9 broadcast_select_fusion.3.refs_1_
  62.3 1.5 collective-permute-start.11
  63.8 1.4 reshape_add_fusion
  68.4 6.5 %collective-permute-done.13.refs_3_ = bf16[2,256,512]{2,1,0:T(8,128)(2,1)} collective-permute-done((bf16[2,256,512]{2,1,0:T(8,128)(2,1)}, bf16[2,256,512]{2,1,0:T(8,128)(2,1)}, u32[]{:S(2)}, u32[]{:S(2)}) %collective-permute-start.13) | collective-permute-done | bytes 524320 | tf_op jit(solution)/shard_map/ppermute | solution.py:679
  74.9 19.0 %shard_map.188 = (f32[1216,512]{1,0:T(8,128)}, f32[1216,512]{1,0:T(8,128)}, f32[1216,128]{1,0:T(8,128)}, bf16[2,256,512]{2,1,0:T(8,128)(2,1)}, bf16[2,256,512]{2...) custom-call(s32[5]{0:T(128)} %stack.88.which_ref, ...), custom_call_target="tpu_custom_call" | custom-call | tf_op jit(solution)/shard_map/pallas_call | solution.py:645
  93.9 20.6 %shard_map.189 = (bf16[2,304,512]{2,1,0:T(8,128)(2,1)}, bf16[304,512]{1,0:T(8,128)(2,1)}, bf16[304,512]{1,0:T(8,128)(2,1)}, bf16[2,304,640]{2,1,0:T(8,128)(2,1)}...) custom-call(s32[5]{0:T(128)} %stack.85.which_ref, ...), custom_call_target="tpu_custom_call" | custom-call | tf_op jit(solution)/shard_map/pallas_call | solution.py:645
  114.6 2.5 collective-permute-done.14.refs_1_
  117.0 1.4 fusion.4
  118.4 1.6 collective-permute-start.15
  122.1 1.5 collective-permute-start.19
  124.7 4.9 %collective-permute-done.15.refs_2_ = bf16[304,640]{1,0:T(8,128)(2,1)S(1)} collective-permute-done((bf16[304,640]{1,0:T(8,128)(2,1)S(1)}, bf16[304,640]{1,0:T(8,128)(2,1)S(1)}, u32[]{:S(2)}, u32[]{:S(2)}) %collective-permute-start.15) | collective-permute-done | bytes 389152 | tf_op jit(solution)/shard_map/ppermute | solution.py:675
  130.3 4.8 %shard_map.190 = (f32[304,512]{1,0:T(8,128)}, bf16[304,512]{1,0:T(8,128)(2,1)}, f32[5,512]{1,0:T(8,128)}) custom-call(s32[2]{0:T(128)} %pad_add_fusion.t_ref.scalars, bf16[304,640]{1,0:T(8,128)(2,1)} %get-tuple-element.104.refs_0_, bf16[2,304,640]{2,1,0:T(8,128)(2,1)} %copy-done.5, bf16[304,640]{1,0:T(8,128)(2,1)} %copy-done.14, ...), custom_call_target="tpu_custom_call" | custom-call | tf_op jit(solution)/shard_map/pallas_call | solution.py:645
  135.1 1.4 collective-permute-done.18
  136.5 11.2 %collective-permute-done.19 = bf16[2,256,512]{2,1,0:T(8,128)(2,1)S(1)} collective-permute-done((bf16[2,256,512]{2,1,0:T(8,128)(2,1)}, bf16[2,256,512]{2,1,0:T(8,128)(2,1)S(1)}, u32[]{:S(2)}, u32[]{:S(2)}) %collective-permute-start.19) | collective-permute-done | bytes 524320 | tf_op jit(solution)/shard_map/ppermute | solution.py:679
  148.3 9.7 %collective-permute-done.21 = bf16[2,256,512]{2,1,0:T(8,128)(2,1)} collective-permute-done((bf16[2,256,512]{2,1,0:T(8,128)(2,1)}, bf16[2,256,512]{2,1,0:T(8,128)(2,1)}, u32[]{:S(2)}, u32[]{:S(2)}) %collective-permute-start.21) | collective-permute-done | bytes 524320 | tf_op jit(solution)/shard_map/ppermute | solution.py:679
  158.0 2.2 broadcast_select_fusion
  161.0 1.6 collective-permute-done.26.g3_ref
  163.3 13.2 %shard_map.191 = (bf16[2,304,512]{2,1,0:T(8,128)(2,1)}, bf16[304,512]{1,0:T(8,128)(2,1)}, bf16[304,512]{1,0:T(8,128)(2,1)}, bf16[2,512,128]{2,1,0:T(8,128)(2,1)}...) custom-call(s32[2]{0:T(128)} %pad_add_fusion.t_ref.scalars, bf16[304,512]{1,0:T(8,128)(2,1)} %get-tuple-element.107.g0_ref, ...), custom_call_target="tpu_custom_call" | custom-call | tf_op jit(solution)/shard_map/pallas_call | solution.py:645
  176.8 2.0 add_convert_fusion.2
  179.8 4.1 %collective-permute-start.23 = (bf16[2,256,512]{2,1,0:T(8,128)(2,1)}, bf16[2,256,512]{2,1,0:T(8,128)(2,1)S(1)}, u32[]{:S(2)}, u32[]{:S(2)}) collective-permute-start(bf16[2,256,512]{2,1,0:T(8,128)(2,1)} %get-tuple-element.158), channel_id=1, source_target_pairs={{0,24},{4,28},{8,0},{12,4},{16,8},{20,12},{24,16},{28,20},{1,25},{... | collective-permute-start | bytes 1572872 | tf_op jit(solution)/shard_map/ppermute | solution.py:679
  186.7 19.3 %collective-permute-done.20 = bf16[2,256,512]{2,1,0:T(8,128)(2,1)} collective-permute-done((bf16[2,256,512]{2,1,0:T(8,128)(2,1)}, bf16[2,256,512]{2,1,0:T(8,128)(2,1)}, u32[]{:S(2)}, u32[]{:S(2)}) %collective-permute-start.20) | collective-permute-done | bytes 524320 | tf_op jit(solution)/shard_map/ppermute | solution.py:679
  206.0 11.8 %collective-permute-done.22 = bf16[2,256,512]{2,1,0:T(8,128)(2,1)S(1)} collective-permute-done((bf16[2,256,512]{2,1,0:T(8,128)(2,1)}, bf16[2,256,512]{2,1,0:T(8,128)(2,1)S(1)}, u32[]{:S(2)}, u32[]{:S(2)}) %collective-permute-start.22) | collective-permute-done | bytes 524320 | tf_op jit(solution)/shard_map/ppermute | solution.py:679
  218.7 1.2 multiply_reduce_fusion
  221.3 10.6 %collective-permute-start.34 = (bf16[2,512,128]{2,1,0:T(8,128)(2,1)S(1)}, bf16[2,512,128]{2,1,0:T(8,128)(2,1)S(1)}, u32[]{:S(2)}, u32[]{:S(2)}) collective-permute-start(bf16[2,512,128]{2,1,0:T(8,128)(2,1)S(1)} %add_convert_fusion.6), channel_id=1, source_target_pairs={{0,8},{4,12},{8,0},{12,4},{16,24},{20,28},{24,16},{28,20},{1,9},{5... | collective-permute-start | bytes 786440 | tf_op jit(solution)/shard_map/ppermute | solution.py:679
  232.7 3.0 %collective-permute-done.30 = f32[9,512]{1,0:T(8,128)S(1)} collective-permute-done((f32[9,512]{1,0:T(8,128)S(1)}, f32[9,512]{1,0:T(8,128)S(1)}, u32[]{:S(2)}, u32[]{:S(2)}) %collective-permute-start.30) | collective-permute-done | bytes 18464 | tf_op jit(solution)/shard_map/ppermute | solution.py:675
  236.5 3.3 %shard_map.192 = bf16[304,512]{1,0:T(8,128)(2,1)} custom-call(s32[2]{0:T(128)} %pad_add_fusion.t_ref.scalars, bf16[304,512]{1,0:T(8,128)(2,1)} %constant_dynamic-slice_fusion.2.refs_0_, bf16[304,512]{1,0:T(8,128)(2,1)} %get-tuple-element.129.refs_1_, bf16[2,304,512]{2,1,0:T(8,128)(2,1)} %copy-done.6, bf16[304,512]{1,0:T(8,128)(2,1)} %copy-done.19, ...), custom_call_target="tpu_custom_call" | custom-call | tf_op jit(solution)/shard_map/pallas_call | solution.py:645
  241.3 3.3 %collective-permute-done.38 = f32[9,512]{1,0:T(8,128)S(1)} collective-permute-done((f32[9,512]{1,0:T(8,128)S(1)}, f32[9,512]{1,0:T(8,128)S(1)}, u32[]{:S(2)}, u32[]{:S(2)}) %collective-permute-start.38) | collective-permute-done | bytes 18464 | tf_op jit(solution)/shard_map/ppermute | solution.py:679
  244.6 3.7 %collective-permute-done.37 = bf16[304,512]{1,0:T(8,128)(2,1)S(1)} collective-permute-done((bf16[304,512]{1,0:T(8,128)(2,1)}, bf16[304,512]{1,0:T(8,128)(2,1)S(1)}, u32[]{:S(2)}, u32[]{:S(2)}) %collective-permute-start.37) | collective-permute-done | bytes 311328 | tf_op jit(solution)/shard_map/ppermute | solution.py:675
  248.8 5.7 %collective-permute-start.42 = (f32[9,512]{1,0:T(8,128)S(1)}, f32[9,512]{1,0:T(8,128)S(1)}, u32[]{:S(2)}, u32[]{:S(2)}) collective-permute-start(f32[9,512]{1,0:T(8,128)S(1)} %add.127), channel_id=1, source_target_pairs={{0,8},{4,12},{8,0},{12,4},{16,24},{20,28},{24,16},{28,20},{1,9},{5... | collective-permute-start | bytes 55304 | tf_op jit(solution)/shard_map/ppermute | solution.py:679
  256.7 1.8 slice_convert_fusion
  258.5 10.4 %collective-permute-done.35 = bf16[2,512,128]{2,1,0:T(8,128)(2,1)S(1)} collective-permute-done((bf16[2,512,128]{2,1,0:T(8,128)(2,1)S(1)}, bf16[2,512,128]{2,1,0:T(8,128)(2,1)S(1)}, u32[]{:S(2)}, u32[]{:S(2)}) %collective-permute-start.35) | collective-permute-done | bytes 262176 | tf_op jit(solution)/shard_map/ppermute | solution.py:679
  269.0 1.5 collective-permute-start.41
  270.6 1.4 add_add_fusion
  276.2 1.4 collective-permute-done.43
  (177 shorter events, 40.9 us)
Async XLA Ops:
  2.8 91.1 %collective-permute-start.10 = (bf16[2,256,512]{2,1,0:T(8,128)(2,1)S(1)}, bf16[2,256,512]{2,1,0:T(8,128)(2,1)}, u32[]{:S(2)}, u32[]{:S(2)}) collective-permute-start(bf16[2,256,512]{2,1,0:T(8,128)(2,1)S(1)} %pad_maximum_fusion.2.refs_0_), channel_id=1, source_target_pairs={{0,4},{4,0},{8,12},{12,8},{16,20},{20,16},{24,28},{28,24},{1,5},{5... | collective-permute-start | bytes 1572872 | tf_op jit(solution)/shard_map/ppermute | solution.py:679
  5.8 16.8 %collective-permute-start.3 = (bf16[2,256,512]{2,1,0:T(8,128)(2,1)S(1)}, bf16[2,256,512]{2,1,0:T(8,128)(2,1)S(1)}, u32[]{:S(2)}, u32[]{:S(2)}) collective-permute-start(bf16[2,256,512]{2,1,0:T(8,128)(2,1)S(1)} %pad_maximum_fusion.2.refs_0_), channel_id=1, source_target_pairs={{8,0},{12,4},{16,8},{20,12},{24,16},{28,20},{9,1},{13,5},{17,9},{2... | collective-permute-start | bytes 1572872 | tf_op jit(solution)/shard_map/ppermute | solution.py:679
  7.1 15.5 %collective-permute-start.2 = (bf16[2,256,512]{2,1,0:T(8,128)(2,1)S(1)}, bf16[2,256,512]{2,1,0:T(8,128)(2,1)S(1)}, u32[]{:S(2)}, u32[]{:S(2)}) collective-permute-start(bf16[2,256,512]{2,1,0:T(8,128)(2,1)S(1)} %pad_maximum_fusion.2.refs_0_), channel_id=1, source_target_pairs={{0,8},{4,12},{8,16},{12,20},{16,24},{20,28},{1,9},{5,13},{9,17},{1... | collective-permute-start | bytes 1572872 | tf_op jit(solution)/shard_map/ppermute | solution.py:679
  20.7 5.4 %collective-permute-start = (bf16[2,304,512]{2,1,0:T(8,128)(2,1)}, bf16[2,304,512]{2,1,0:T(8,128)(2,1)S(1)}, u32[]{:S(2)}, u32[]{:S(2)}) collective-permute-start(bf16[2,304,512]{2,1,0:T(8,128)(2,1)} %get-tuple-element.83), channel_id=1, source_target_pairs={{0,1},{1,0},{2,3},{3,2},{4,5},{5,4},{6,7},{7,6},{8,9},{9,8},{10,11... | collective-permute-start | bytes 1867784 | tf_op jit(solution)/shard_map/ppermute | solution.py:671
  22.6 6.3 %collective-permute-start.4 = (bf16[2,256,512]{2,1,0:T(8,128)(2,1)S(1)}, bf16[2,256,512]{2,1,0:T(8,128)(2,1)}, u32[]{:S(2)}, u32[]{:S(2)}) collective-permute-start(bf16[2,256,512]{2,1,0:T(8,128)(2,1)S(1)} %collective-permute-done.2), channel_id=1, source_target_pairs={{8,16},{12,20},{16,24},{20,28},{9,17},{13,21},{17,25},{21,29},{10,... | collective-permute-start | bytes 1572872 | tf_op jit(solution)/shard_map/ppermute | solution.py:679
  24.1 18.7 %collective-permute-start.5 = (bf16[2,256,512]{2,1,0:T(8,128)(2,1)S(1)}, bf16[2,256,512]{2,1,0:T(8,128)(2,1)}, u32[]{:S(2)}, u32[]{:S(2)}) collective-permute-start(bf16[2,256,512]{2,1,0:T(8,128)(2,1)S(1)} %collective-permute-done.3), channel_id=1, source_target_pairs={{8,0},{12,4},{16,8},{20,12},{9,1},{13,5},{17,9},{21,13},{10,2},{14... | collective-permute-start | bytes 1572872 | tf_op jit(solution)/shard_map/ppermute | solution.py:679
  27.4 21.0 %collective-permute-start.1 = (bf16[304,512]{1,0:T(8,128)(2,1)S(1)}, bf16[304,512]{1,0:T(8,128)(2,1)}, u32[]{:S(2)}, u32[]{:S(2)}) collective-permute-start(bf16[304,512]{1,0:T(8,128)(2,1)S(1)} %fusion.8), channel_id=1, source_target_pairs={{0,2},{1,3},{2,0},{3,1},{4,6},{5,7},{6,4},{7,5},{8,10},{9,11},{10,... | collective-permute-start | bytes 933896 | tf_op jit(solution)/shard_map/ppermute | solution.py:675
  44.7 15.1 %collective-permute-start.8 = (bf16[2,256,512]{2,1,0:T(8,128)(2,1)}, bf16[2,256,512]{2,1,0:T(8,128)(2,1)}, u32[]{:S(2)}, u32[]{:S(2)}) collective-permute-start(bf16[2,256,512]{2,1,0:T(8,128)(2,1)} %broadcast_select_fusion.4.refs_1_), channel_id=1, source_target_pairs={{16,24},{20,28},{8,0},{12,4},{17,25},{21,29},{9,1},{13,5},{18,26},... | collective-permute-start | bytes 1572872 | tf_op jit(solution)/shard_map/ppermute | solution.py:679
  47.0 16.7 %collective-permute-start.12 = (bf16[2,256,512]{2,1,0:T(8,128)(2,1)}, bf16[2,256,512]{2,1,0:T(8,128)(2,1)}, u32[]{:S(2)}, u32[]{:S(2)}) collective-permute-start(bf16[2,256,512]{2,1,0:T(8,128)(2,1)} %broadcast_select_fusion.2.refs_0_), channel_id=1, source_target_pairs={{0,4},{4,0},{8,12},{12,8},{16,20},{20,16},{24,28},{28,24},{1,5},{5... | collective-permute-start | bytes 1572872 | tf_op jit(solution)/shard_map/ppermute | solution.py:679
  51.7 10.5 %collective-permute-start.7 = (bf16[304,512]{1,0:T(8,128)(2,1)}, bf16[304,512]{1,0:T(8,128)(2,1)}, u32[]{:S(2)}, u32[]{:S(2)}) collective-permute-start(bf16[304,512]{1,0:T(8,128)(2,1)} %get-tuple-element.91.x0_ref), channel_id=1, source_target_pairs={{0,2},{1,3},{2,0},{3,1},{4,6},{5,7},{6,4},{7,5},{8,10},{9,11},{10,... | collective-permute-start | bytes 933896 | tf_op jit(solution)/shard_map/ppermute | solution.py:675
  55.3 13.1 %collective-permute-start.6 = (bf16[304,512]{1,0:T(8,128)(2,1)}, bf16[304,512]{1,0:T(8,128)(2,1)}, u32[]{:S(2)}, u32[]{:S(2)}) collective-permute-start(bf16[304,512]{1,0:T(8,128)(2,1)} %get-tuple-element.91.x0_ref), channel_id=1, source_target_pairs={{0,1},{1,0},{2,3},{3,2},{4,5},{5,4},{6,7},{7,6},{8,9},{9,8},{10,11... | collective-permute-start | bytes 933896 | tf_op jit(solution)/shard_map/ppermute | solution.py:671
  59.8 15.1 %collective-permute-start.13 = (bf16[2,256,512]{2,1,0:T(8,128)(2,1)}, bf16[2,256,512]{2,1,0:T(8,128)(2,1)}, u32[]{:S(2)}, u32[]{:S(2)}) collective-permute-start(bf16[2,256,512]{2,1,0:T(8,128)(2,1)} %broadcast_select_fusion.4.refs_1_), channel_id=1, source_target_pairs={{0,4},{4,0},{8,12},{12,8},{16,20},{20,16},{24,28},{28,24},{1,5},{5... | collective-permute-start | bytes 1572872 | tf_op jit(solution)/shard_map/ppermute | solution.py:679
  62.3 31.7 %collective-permute-start.11 = (bf16[2,256,512]{2,1,0:T(8,128)(2,1)}, bf16[2,256,512]{2,1,0:T(8,128)(2,1)}, u32[]{:S(2)}, u32[]{:S(2)}) collective-permute-start(bf16[2,256,512]{2,1,0:T(8,128)(2,1)} %broadcast_select_fusion.3.refs_1_), channel_id=1, source_target_pairs={{0,4},{4,0},{8,12},{12,8},{16,20},{20,16},{24,28},{28,24},{1,5},{5... | collective-permute-start | bytes 1572872 | tf_op jit(solution)/shard_map/ppermute | solution.py:679
  63.8 11.2 %collective-permute-start.9 = (bf16[304,512]{1,0:T(8,128)(2,1)}, bf16[304,512]{1,0:T(8,128)(2,1)}, u32[]{:S(2)}, u32[]{:S(2)}) collective-permute-start(bf16[304,512]{1,0:T(8,128)(2,1)} %collective-permute-done.7.x2_ref), channel_id=1, source_target_pairs={{0,1},{1,0},{2,3},{3,2},{4,5},{5,4},{6,7},{7,6},{8,9},{9,8},{10,11... | collective-permute-start | bytes 933896 | tf_op jit(solution)/shard_map/ppermute | solution.py:671
  114.5 2.5 collective-permute-start.14
  118.4 11.1 %collective-permute-start.15 = (bf16[304,640]{1,0:T(8,128)(2,1)S(1)}, bf16[304,640]{1,0:T(8,128)(2,1)S(1)}, u32[]{:S(2)}, u32[]{:S(2)}) collective-permute-start(bf16[304,640]{1,0:T(8,128)(2,1)S(1)} %fusion.4), channel_id=1, source_target_pairs={{0,2},{1,3},{2,0},{3,1},{4,6},{5,7},{6,4},{7,5},{8,10},{9,11},{10,... | collective-permute-start | bytes 1167368 | tf_op jit(solution)/shard_map/ppermute | solution.py:675
  121.5 15.0 %collective-permute-start.18 = (bf16[2,256,512]{2,1,0:T(8,128)(2,1)}, bf16[2,256,512]{2,1,0:T(8,128)(2,1)S(1)}, u32[]{:S(2)}, u32[]{:S(2)}) collective-permute-start(bf16[2,256,512]{2,1,0:T(8,128)(2,1)} %get-tuple-element.111), channel_id=1, source_target_pairs={{0,4},{4,0},{8,12},{12,8},{16,20},{20,16},{24,28},{28,24},{1,5},{5... | collective-permute-start | bytes 1572872 | tf_op jit(solution)/shard_map/ppermute | solution.py:679
  122.1 25.7 %collective-permute-start.19 = (bf16[2,256,512]{2,1,0:T(8,128)(2,1)}, bf16[2,256,512]{2,1,0:T(8,128)(2,1)S(1)}, u32[]{:S(2)}, u32[]{:S(2)}) collective-permute-start(bf16[2,256,512]{2,1,0:T(8,128)(2,1)} %get-tuple-element.112), channel_id=1, source_target_pairs={{0,4},{4,0},{8,12},{12,8},{16,20},{20,16},{24,28},{28,24},{1,5},{5... | collective-permute-start | bytes 1572872 | tf_op jit(solution)/shard_map/ppermute | solution.py:679
  123.5 34.4 %collective-permute-start.21 = (bf16[2,256,512]{2,1,0:T(8,128)(2,1)}, bf16[2,256,512]{2,1,0:T(8,128)(2,1)}, u32[]{:S(2)}, u32[]{:S(2)}) collective-permute-start(bf16[2,256,512]{2,1,0:T(8,128)(2,1)} %get-tuple-element.119), channel_id=1, source_target_pairs={{0,4},{4,0},{8,12},{12,8},{16,20},{20,16},{24,28},{28,24},{1,5},{5... | collective-permute-start | bytes 1572872 | tf_op jit(solution)/shard_map/ppermute | solution.py:679
  135.1 25.1 %collective-permute-start.16 = (bf16[2,304,512]{2,1,0:T(8,128)(2,1)}, bf16[2,304,512]{2,1,0:T(8,128)(2,1)S(1)}, u32[]{:S(2)}, u32[]{:S(2)}) collective-permute-start(bf16[2,304,512]{2,1,0:T(8,128)(2,1)} %get-tuple-element.108), channel_id=1, source_target_pairs={{0,1},{1,0},{2,3},{3,2},{4,5},{5,4},{6,7},{7,6},{8,9},{9,8},{10,11... | collective-permute-start | bytes 1867784 | tf_op jit(solution)/shard_map/ppermute | solution.py:671
  136.5 40.1 %copy-start.12 = (bf16[2,256,512]{2,1,0:T(8,128)(2,1)}, bf16[2,256,512]{2,1,0:T(8,128)(2,1)S(1)}, u32[]{:S(2)}) copy-start(bf16[2,256,512]{2,1,0:T(8,128)(2,1)S(1)} %collective-permute-done.18) | copy-start | bytes 1572868
  147.8 13.2 %collective-permute-start.25 = (bf16[304,512]{1,0:T(8,128)(2,1)}, bf16[304,512]{1,0:T(8,128)(2,1)S(1)}, u32[]{:S(2)}, u32[]{:S(2)}) collective-permute-start(bf16[304,512]{1,0:T(8,128)(2,1)} %get-tuple-element.107.g0_ref), channel_id=1, source_target_pairs={{0,2},{1,3},{2,0},{3,1},{4,6},{5,7},{6,4},{7,5},{8,10},{9,11},{10,... | collective-permute-start | bytes 933896 | tf_op jit(solution)/shard_map/ppermute | solution.py:675
  148.3 12.7 %collective-permute-start.24 = (bf16[304,512]{1,0:T(8,128)(2,1)}, bf16[304,512]{1,0:T(8,128)(2,1)S(1)}, u32[]{:S(2)}, u32[]{:S(2)}) collective-permute-start(bf16[304,512]{1,0:T(8,128)(2,1)} %get-tuple-element.107.g0_ref), channel_id=1, source_target_pairs={{0,1},{1,0},{2,3},{3,2},{4,5},{5,4},{6,7},{7,6},{8,9},{9,8},{10,11... | collective-permute-start | bytes 933896 | tf_op jit(solution)/shard_map/ppermute | solution.py:671
  161.0 1.6 collective-permute-start.26
  176.6 8.7 %collective-permute-start.27 = (bf16[2,304,512]{2,1,0:T(8,128)(2,1)}, bf16[2,304,512]{2,1,0:T(8,128)(2,1)S(1)}, u32[]{:S(2)}, u32[]{:S(2)}) collective-permute-start(bf16[2,304,512]{2,1,0:T(8,128)(2,1)} %get-tuple-element.127), channel_id=1, source_target_pairs={{0,1},{1,0},{2,3},{3,2},{4,5},{5,4},{6,7},{7,6},{8,9},{9,8},{10,11... | collective-permute-start | bytes 1867784 | tf_op jit(solution)/shard_map/ppermute | solution.py:671
  178.8 39.9 %copy-start.2 = (f32[304,512]{1,0:T(8,128)S(1)}, f32[304,512]{1,0:T(8,128)}, u32[]{:S(2)}) copy-start(f32[304,512]{1,0:T(8,128)} %get-tuple-element.90.refs_3_) | copy-start | bytes 1867780
  178.8 27.2 %collective-permute-start.20 = (bf16[2,256,512]{2,1,0:T(8,128)(2,1)}, bf16[2,256,512]{2,1,0:T(8,128)(2,1)}, u32[]{:S(2)}, u32[]{:S(2)}) collective-permute-start(bf16[2,256,512]{2,1,0:T(8,128)(2,1)} %add_convert_fusion.2), channel_id=1, source_target_pairs={{0,16},{4,20},{8,24},{12,28},{16,0},{20,4},{24,8},{28,12},{1,17},{... | collective-permute-start | bytes 1572872 | tf_op jit(solution)/shard_map/ppermute | solution.py:679
  179.8 26.3 %collective-permute-start.23 = (bf16[2,256,512]{2,1,0:T(8,128)(2,1)}, bf16[2,256,512]{2,1,0:T(8,128)(2,1)S(1)}, u32[]{:S(2)}, u32[]{:S(2)}) collective-permute-start(bf16[2,256,512]{2,1,0:T(8,128)(2,1)} %get-tuple-element.158), channel_id=1, source_target_pairs={{0,24},{4,28},{8,0},{12,4},{16,8},{20,12},{24,16},{28,20},{1,25},{... | collective-permute-start | bytes 1572872 | tf_op jit(solution)/shard_map/ppermute | solution.py:679
  183.9 34.0 %collective-permute-start.22 = (bf16[2,256,512]{2,1,0:T(8,128)(2,1)}, bf16[2,256,512]{2,1,0:T(8,128)(2,1)S(1)}, u32[]{:S(2)}, u32[]{:S(2)}) collective-permute-start(bf16[2,256,512]{2,1,0:T(8,128)(2,1)} %broadcast_select_fusion.1), channel_id=1, source_target_pairs={{0,8},{4,12},{8,16},{12,20},{16,24},{20,28},{24,0},{28,4},{1,9},{5... | collective-permute-start | bytes 1572872 | tf_op jit(solution)/shard_map/ppermute | solution.py:679
  183.9 34.0 %collective-permute-start.17 = (bf16[304,512]{1,0:T(8,128)(2,1)}, bf16[304,512]{1,0:T(8,128)(2,1)S(1)}, u32[]{:S(2)}, u32[]{:S(2)}) collective-permute-start(bf16[304,512]{1,0:T(8,128)(2,1)} %fusion.6), channel_id=1, source_target_pairs={{0,2},{1,3},{2,0},{3,1},{4,6},{5,7},{6,4},{7,5},{8,10},{9,11},{10,... | collective-permute-start | bytes 933896 | tf_op jit(solution)/shard_map/ppermute | solution.py:675
  185.3 34.5 %copy-start.6 = (bf16[2,304,512]{2,1,0:T(8,128)(2,1)}, bf16[2,304,512]{2,1,0:T(8,128)(2,1)S(1)}, u32[]{:S(2)}) copy-start(bf16[2,304,512]{2,1,0:T(8,128)(2,1)S(1)} %collective-permute-done.27.refs_2_) | copy-start | bytes 1867780
  185.3 35.9 %collective-permute-start.31 = (bf16[2,512,128]{2,1,0:T(8,128)(2,1)}, bf16[2,512,128]{2,1,0:T(8,128)(2,1)S(1)}, u32[]{:S(2)}, u32[]{:S(2)}) collective-permute-start(bf16[2,512,128]{2,1,0:T(8,128)(2,1)} %get-tuple-element.134), channel_id=1, source_target_pairs={{0,4},{4,0},{8,12},{12,8},{16,20},{20,16},{24,28},{28,24},{1,5},{5... | collective-permute-start | bytes 786440 | tf_op jit(solution)/shard_map/ppermute | solution.py:679
  219.9 1.3 collective-permute-start.29
  219.9 15.8 %collective-permute-start.28 = (bf16[304,512]{1,0:T(8,128)(2,1)S(1)}, bf16[304,512]{1,0:T(8,128)(2,1)S(1)}, u32[]{:S(2)}, u32[]{:S(2)}) collective-permute-start(bf16[304,512]{1,0:T(8,128)(2,1)S(1)} %fusion.5), channel_id=1, source_target_pairs={{0,2},{1,3},{2,0},{3,1},{4,6},{5,7},{6,4},{7,5},{8,10},{9,11},{10,... | collective-permute-start | bytes 933896 | tf_op jit(solution)/shard_map/ppermute | solution.py:675
  221.3 19.9 %collective-permute-start.34 = (bf16[2,512,128]{2,1,0:T(8,128)(2,1)S(1)}, bf16[2,512,128]{2,1,0:T(8,128)(2,1)S(1)}, u32[]{:S(2)}, u32[]{:S(2)}) collective-permute-start(bf16[2,512,128]{2,1,0:T(8,128)(2,1)S(1)} %add_convert_fusion.6), channel_id=1, source_target_pairs={{0,8},{4,12},{8,0},{12,4},{16,24},{20,28},{24,16},{28,20},{1,9},{5... | collective-permute-start | bytes 786440 | tf_op jit(solution)/shard_map/ppermute | solution.py:679
  231.8 3.9 %collective-permute-start.30 = (f32[9,512]{1,0:T(8,128)S(1)}, f32[9,512]{1,0:T(8,128)S(1)}, u32[]{:S(2)}, u32[]{:S(2)}) collective-permute-start(f32[9,512]{1,0:T(8,128)S(1)} %fusion.18), channel_id=1, source_target_pairs={{0,2},{1,3},{2,0},{3,1},{4,6},{5,7},{6,4},{7,5},{8,10},{9,11},{10,... | collective-permute-start | bytes 55304 | tf_op jit(solution)/shard_map/ppermute | solution.py:675
  239.8 8.5 %collective-permute-start.37 = (bf16[304,512]{1,0:T(8,128)(2,1)}, bf16[304,512]{1,0:T(8,128)(2,1)S(1)}, u32[]{:S(2)}, u32[]{:S(2)}) collective-permute-start(bf16[304,512]{1,0:T(8,128)(2,1)} %shard_map.192), channel_id=1, source_target_pairs={{0,2},{1,3},{2,0},{3,1},{4,6},{5,7},{6,4},{7,5},{8,10},{9,11},{10,... | collective-permute-start | bytes 933896 | tf_op jit(solution)/shard_map/ppermute | solution.py:675
  240.7 3.9 %collective-permute-start.38 = (f32[9,512]{1,0:T(8,128)S(1)}, f32[9,512]{1,0:T(8,128)S(1)}, u32[]{:S(2)}, u32[]{:S(2)}) collective-permute-start(f32[9,512]{1,0:T(8,128)S(1)} %add.125), channel_id=1, source_target_pairs={{0,4},{4,0},{8,12},{12,8},{16,20},{20,16},{24,28},{28,24},{1,5},{5... | collective-permute-start | bytes 55304 | tf_op jit(solution)/shard_map/ppermute | solution.py:679
  241.2 13.3 %collective-permute-start.36 = (bf16[304,512]{1,0:T(8,128)(2,1)}, bf16[304,512]{1,0:T(8,128)(2,1)S(1)}, u32[]{:S(2)}, u32[]{:S(2)}) collective-permute-start(bf16[304,512]{1,0:T(8,128)(2,1)} %shard_map.192), channel_id=1, source_target_pairs={{0,1},{1,0},{2,3},{3,2},{4,5},{5,4},{6,7},{7,6},{8,9},{9,8},{10,11... | collective-permute-start | bytes 933896 | tf_op jit(solution)/shard_map/ppermute | solution.py:671
  248.3 6.8 %collective-permute-start.39 = (bf16[304,512]{1,0:T(8,128)(2,1)S(1)}, bf16[304,512]{1,0:T(8,128)(2,1)S(1)}, u32[]{:S(2)}, u32[]{:S(2)}) collective-permute-start(bf16[304,512]{1,0:T(8,128)(2,1)S(1)} %collective-permute-done.37), channel_id=1, source_target_pairs={{0,1},{1,0},{2,3},{3,2},{4,5},{5,4},{6,7},{7,6},{8,9},{9,8},{10,11... | collective-permute-start | bytes 933896 | tf_op jit(solution)/shard_map/ppermute | solution.py:671
  248.3 22.3 %collective-permute-start.44 = (bf16[2,256,512]{2,1,0:T(8,128)(2,1)}, bf16[2,256,512]{2,1,0:T(8,128)(2,1)S(1)}, u32[]{:S(2)}, u32[]{:S(2)}) collective-permute-start(bf16[2,256,512]{2,1,0:T(8,128)(2,1)} %get-tuple-element.149), channel_id=1, source_target_pairs={{0,4},{4,0},{8,12},{12,8},{16,20},{20,16},{24,28},{28,24},{1,5},{5... | collective-permute-start | bytes 1572872 | tf_op jit(solution)/shard_map/ppermute | solution.py:679
  248.8 23.1 %collective-permute-start.42 = (f32[9,512]{1,0:T(8,128)S(1)}, f32[9,512]{1,0:T(8,128)S(1)}, u32[]{:S(2)}, u32[]{:S(2)}) collective-permute-start(f32[9,512]{1,0:T(8,128)S(1)} %add.127), channel_id=1, source_target_pairs={{0,8},{4,12},{8,0},{12,4},{16,24},{20,28},{24,16},{28,20},{1,9},{5... | collective-permute-start | bytes 55304 | tf_op jit(solution)/shard_map/ppermute | solution.py:679
  254.5 14.4 %collective-permute-start.35 = (bf16[2,512,128]{2,1,0:T(8,128)(2,1)S(1)}, bf16[2,512,128]{2,1,0:T(8,128)(2,1)S(1)}, u32[]{:S(2)}, u32[]{:S(2)}) collective-permute-start(bf16[2,512,128]{2,1,0:T(8,128)(2,1)S(1)} %add_convert_fusion.5), channel_id=1, source_target_pairs={{0,16},{4,20},{8,24},{12,28},{16,0},{20,4},{24,8},{28,12},{1,17},{... | collective-permute-start | bytes 786440 | tf_op jit(solution)/shard_map/ppermute | solution.py:679
  254.5 18.3 %collective-permute-start.33 = (bf16[304,512]{1,0:T(8,128)(2,1)S(1)}, bf16[304,512]{1,0:T(8,128)(2,1)S(1)}, u32[]{:S(2)}, u32[]{:S(2)}) collective-permute-start(bf16[304,512]{1,0:T(8,128)(2,1)S(1)} %get-tuple-element.139), channel_id=1, source_target_pairs={{0,2},{1,3},{2,0},{3,1},{4,6},{5,7},{6,4},{7,5},{8,10},{9,11},{10,... | collective-permute-start | bytes 933896 | tf_op jit(solution)/shard_map/ppermute | solution.py:675
  255.0 18.7 %collective-permute-start.32 = (bf16[304,512]{1,0:T(8,128)(2,1)S(1)}, bf16[304,512]{1,0:T(8,128)(2,1)S(1)}, u32[]{:S(2)}, u32[]{:S(2)}) collective-permute-start(bf16[304,512]{1,0:T(8,128)(2,1)S(1)} %get-tuple-element.139), channel_id=1, source_target_pairs={{0,1},{1,0},{2,3},{3,2},{4,5},{5,4},{6,7},{7,6},{8,9},{9,8},{10,11... | collective-permute-start | bytes 933896 | tf_op jit(solution)/shard_map/ppermute | solution.py:671
  269.0 10.0 %collective-permute-start.41 = (bf16[2,512,128]{2,1,0:T(8,128)(2,1)S(1)}, bf16[2,512,128]{2,1,0:T(8,128)(2,1)S(1)}, u32[]{:S(2)}, u32[]{:S(2)}) collective-permute-start(bf16[2,512,128]{2,1,0:T(8,128)(2,1)S(1)} %add_convert_fusion.4), channel_id=1, source_target_pairs={{0,4},{4,0},{8,12},{12,8},{16,20},{20,16},{24,28},{28,24},{1,5},{5... | collective-permute-start | bytes 786440 | tf_op jit(solution)/shard_map/ppermute | solution.py:679
  272.8 4.8 %collective-permute-start.43 = (f32[9,512]{1,0:T(8,128)S(1)}, f32[9,512]{1,0:T(8,128)S(1)}, u32[]{:S(2)}, u32[]{:S(2)}) collective-permute-start(f32[9,512]{1,0:T(8,128)S(1)} %add.129), channel_id=1, source_target_pairs={{0,16},{4,20},{8,24},{12,28},{16,0},{20,4},{24,8},{28,12},{1,17},{... | collective-permute-start | bytes 55304 | tf_op jit(solution)/shard_map/ppermute | solution.py:679
  272.8 1.6 collective-permute-start.40
  (26 other events, 297.8 us)
